TPU v7x, 256 devices: a whole 4x4x8 slice. The times are simulated.
256 devices in a mesh: batch: 8 (over z_lo, core), seq: 32 (over y, z_hi, x).
Axes of the slice: x: 4, y: 4, z: 8 (z_hi: 2, z_lo: 4; z = z_hi * 4 + z_lo), core: 2. Of those that a mesh axis runs over, the one named last changes fastest.
Arguments:
- token_ids: int32 [8, 8192], P('batch', 'seq'), may hold values from 0 to 3
- complement: int32 [4], replicated, may hold values from 0 to 3, each once
- embedding: bfloat16 [4, 1024], replicated, may hold values from -6 to 6
- in_weight: bfloat16 [1024, 2176], replicated, may hold values from -0.1875 to 0.1875
- step_weight: bfloat16 [1024, 16], replicated, may hold values from -0.1875 to 0.1875
- conv_weight: float32 [2, 4, 1152], replicated, may hold values from -3 to 3
- conv_bias: float32 [2, 1152], replicated, may hold values from -3 to 3
- step_bias: float32 [2, 16], replicated, may hold values from -4 to -2
- decay_rate: float32 [2, 16], replicated, as said below
- skip_gain: float32 [2, 16], replicated, may hold values from 0.5 to 1.5
- norm_gain: float32 [2, 1024], replicated, may hold values from 0.1 to 1.9
- out_weight: bfloat16 [1024, 1024], P('seq', 'batch'), may hold values from -0.1875 to 0.1875
Outputs:
- mixer_output: bfloat16 [8, 8192, 1024], P('batch', 'seq')
Inputs may be any that keep to these rules, and one draw needn't show every extreme that they name: `decay_rate`: positive decay rate of each head.
All inputs are finite; a program needn't handle non-finite values.
Results may differ from a plain program's by a relative error of at most 0.0084.
Values may be sent and summed in bfloat16 or wider, within the bound.
A program may use at most 192 MiB of HBM per device.

v0:
```python
from functools import partial

import jax
import jax.numpy as jnp
from jax import lax
from jax.sharding import PartitionSpec as P

E = 1024
H = 16
HEADDIM = 64
N = 64
BLOCK = 256


exact_mode = lax.Precision.HIGHEST
norm_epsilon = 1e-05


def entering_2(value, axis, combine, identity, reverse):
    length, here = (lax.axis_size(axis), lax.axis_index(axis))
    everything = jax.tree.map(lambda part: lax.all_gather(part, axis), value)
    start = jax.tree.map(
        lambda part, zero: jnp.broadcast_to(jnp.asarray(zero, part.dtype), part.shape),
        value,
        identity,
    )

    def hop(k, before):
        at = length - 1 - k if reverse else k
        reached = at > here if reverse else at < here
        new = combine(before, jax.tree.map(lambda part: part[at], everything))
        return jax.tree.map(lambda a, b: jnp.where(reached, a, b), new, before)

    return lax.fori_loop(0, length, hop, start)


def from_partner(block, axis, stride):
    count = lax.axis_size(axis)
    route = []
    for low in range(count):
        high = low | 1 << stride
        if high != low and high < count:
            route += [(low, high), (high, low)]
    return lax.ppermute(block, axis, route)


def extended(block, sides, width):
    for axis, dim in sides:
        count = lax.axis_size(axis)
        forward = [(i, i + 1) for i in range(count - 1)]
        backward = [(target, source) for source, target in forward]
        low = lax.ppermute(
            lax.slice_in_dim(block, block.shape[dim] - width, None, axis=dim), axis, forward
        )
        high = lax.ppermute(lax.slice_in_dim(block, 0, width, axis=dim), axis, backward)
        block = jnp.concatenate([low, block, high], axis=dim)
    return block


def block_step(carry_state, inputs):
    values, b_rows, c_rows, step_sizes, decays = inputs
    running = jnp.cumsum(decays, axis=1)
    spread = running[:, :, None] - running[:, None, :]
    positions = jnp.arange(running.shape[1])
    lower_mask = positions[:, None] >= positions[None, :]
    weights = jnp.exp(jnp.where(lower_mask[None], spread, -jnp.inf))
    scores = jnp.dot(
        c_rows.astype(jnp.bfloat16),
        b_rows.astype(jnp.bfloat16).T,
        preferred_element_type=jnp.float32,
    )
    mixing = weights * scores[None] * step_sizes[:, None, :]
    inside = jnp.einsum("hts,shp->thp", mixing, values, precision=exact_mode)
    carried = jnp.einsum("tn,hpn->thp", c_rows, carry_state, precision=exact_mode)
    carried = carried * jnp.exp(running).T[:, :, None]
    to_end = jnp.exp(running[:, -1:] - running) * step_sizes
    fresh_state = jnp.einsum("hs,shp,sn->hpn", to_end, values, b_rows, precision=exact_mode)
    carry_state = carry_state * jnp.exp(running[:, -1])[:, None, None] + fresh_state
    return (carry_state, inside + carried)


def state_scan(values, b_rows, c_rows, step_sizes, decays, block_rows):
    length, head_count, head_width = values.shape
    block_count = length // block_rows
    blocks = (
        values.reshape(block_count, block_rows, head_count, head_width),
        b_rows.reshape(block_count, block_rows, -1),
        c_rows.reshape(block_count, block_rows, -1),
        step_sizes.reshape(block_count, block_rows, head_count).transpose(0, 2, 1),
        decays.reshape(block_count, block_rows, head_count).transpose(0, 2, 1),
    )
    start_state = jnp.zeros((head_count, head_width, b_rows.shape[1]), jnp.float32)
    final_state, outputs = lax.scan(block_step, start_state, blocks)
    return (final_state, outputs.reshape(length, head_count, head_width))


def chain_combine(earlier, later):
    decay_early, state_early = earlier
    decay_late, state_late = later
    return (decay_early * decay_late, decay_late[..., None, None] * state_early + state_late)


def gated_norm(outputs, gate_rows, gain_rows):
    gated = outputs * jax.nn.silu(gate_rows.astype(jnp.float32))
    scale = lax.rsqrt(jnp.mean(gated * gated, axis=-1, keepdims=True) + norm_epsilon)
    return gated * scale * gain_rows[:, None, :]


def complement_of(nucleotides, complement, letters):
    matches = nucleotides[..., None] == letters
    return jnp.sum(jnp.where(matches, complement, 0), axis=-1)


def direction_pass(
    padded, step_raw, conv_weight, conv_bias, step_bias, decay_rate, skip_gain, param_sets, falling
):
    streams, local_len, head_count = step_raw.shape
    kernel = conv_weight.shape[1]
    weight_rows = jnp.stack([conv_weight[set_index] for set_index in param_sets])
    bias_rows = jnp.stack([conv_bias[set_index] for set_index in param_sets])
    step_rows = jnp.stack([step_bias[set_index] for set_index in param_sets])
    rate_rows = jnp.stack([decay_rate[set_index] for set_index in param_sets])
    skip_rows = jnp.stack([skip_gain[set_index] for set_index in param_sets])
    if falling:
        window = jnp.flip(padded[:, kernel - 1 :], axis=1)
        raw_steps = jnp.flip(step_raw, axis=1)
    else:
        window = padded[:, : local_len + kernel - 1]
        raw_steps = step_raw
    conv_total = bias_rows[:, None, :]
    for offset in range(kernel):
        conv_total = conv_total + weight_rows[:, offset][:, None, :] * window[
            :, offset : offset + local_len
        ].astype(jnp.float32)
    conved = jax.nn.silu(conv_total).astype(jnp.bfloat16)
    values = conved[..., :E].astype(jnp.float32).reshape(streams, local_len, H, HEADDIM)
    b_rows = conved[..., E : E + N].astype(jnp.float32)
    c_rows = conved[..., E + N :].astype(jnp.float32)
    step_sizes = jax.nn.softplus(raw_steps + step_rows[:, None, :])
    decays = -rate_rows[:, None, :] * step_sizes
    end_state, outputs = jax.vmap(partial(state_scan, block_rows=BLOCK))(
        values, b_rows, c_rows, step_sizes, decays
    )
    running = jnp.cumsum(decays, axis=1)
    total_decay = jnp.exp(running[:, -1])
    identity = (jnp.ones_like(total_decay), jnp.zeros_like(end_state))
    if falling:
        enter_decay, enter_state = entering_2(
            (total_decay, end_state), "seq", chain_combine, identity, True
        )
    else:
        enter_decay, enter_state = entering_2(
            (total_decay, end_state), "seq", chain_combine, identity, False
        )
    entering = jnp.einsum("stn,shpn->sthp", c_rows, enter_state, precision=exact_mode)
    outputs = outputs + entering * jnp.exp(running)[..., None]
    outputs = outputs + skip_rows[:, None, :, None] * values
    outputs = outputs.reshape(streams, local_len, E)
    if falling:
        outputs = jnp.flip(outputs, axis=1)
    return outputs


def on_device(
    token_ids,
    complement,
    embedding,
    in_weight,
    step_weight,
    conv_weight,
    conv_bias,
    step_bias,
    decay_rate,
    skip_gain,
    norm_gain,
    out_weight,
):
    genomes, local_len = token_ids.shape
    bit_count = lax.axis_size("seq").bit_length() - 1
    letters = jnp.arange(embedding.shape[0])
    mirrored = token_ids
    for bit_index in range(bit_count):
        mirrored = from_partner(mirrored, "seq", bit_index)
    other_ids = jnp.flip(complement_of(mirrored, complement, letters), axis=1)
    rising_sets = [0] * (2 * genomes)
    falling_sets = [1] * (2 * genomes)
    strands = jnp.concatenate([token_ids, other_ids], axis=0)
    streams = strands.shape[0]
    one_hot = (strands.reshape(-1)[:, None] == letters[None, :]).astype(jnp.bfloat16)
    strand_rows = jnp.dot(one_hot, embedding, preferred_element_type=jnp.float32).astype(
        jnp.bfloat16
    )
    projected = jnp.dot(strand_rows, in_weight, preferred_element_type=jnp.float32).astype(
        jnp.bfloat16
    )
    projected = projected.reshape(streams, local_len, -1)
    gate_rows = projected[..., :E]
    conv_input = projected[..., E:]
    step_raw = jnp.dot(strand_rows, step_weight, preferred_element_type=jnp.float32).reshape(
        streams, local_len, -1
    )
    rim_width = conv_weight.shape[1] - 1
    padded = extended(conv_input, (("seq", 1),), rim_width)
    rising = direction_pass(
        padded,
        step_raw,
        conv_weight,
        conv_bias,
        step_bias,
        decay_rate,
        skip_gain,
        rising_sets,
        False,
    )
    rising_normed = gated_norm(
        rising, gate_rows, jnp.stack([norm_gain[set_index] for set_index in rising_sets])
    )
    falling = direction_pass(
        padded,
        step_raw,
        conv_weight,
        conv_bias,
        step_bias,
        decay_rate,
        skip_gain,
        falling_sets,
        True,
    )
    falling_normed = gated_norm(
        falling, gate_rows, jnp.stack([norm_gain[set_index] for set_index in falling_sets])
    )
    mixed_rows = (
        (rising_normed + falling_normed).astype(jnp.bfloat16).reshape(streams * local_len, E)
    )
    columns = lax.all_gather(out_weight, "batch", axis=1, tiled=True)
    strand_out = jnp.dot(
        mixed_rows,
        lax.all_gather(columns, "seq", axis=0, tiled=True),
        preferred_element_type=jnp.float32,
    )
    strand_out = strand_out.astype(jnp.bfloat16).reshape(streams, local_len, -1)
    forward_part = strand_out[:genomes]
    other_part = strand_out[genomes:]
    for bit_index in range(bit_count):
        other_part = from_partner(other_part, "seq", bit_index)
    other_part = jnp.flip(other_part, axis=1)
    return (forward_part.astype(jnp.float32) + other_part.astype(jnp.float32)).astype(jnp.bfloat16)


def solution(mesh):
    placed = (
        P("batch", "seq"),
        P(),
        P(),
        P(),
        P(),
        P(),
        P(),
        P(),
        P(),
        P(),
        P(),
        P("seq", "batch"),
    )
    return jax.shard_map(
        on_device, mesh=mesh, in_specs=placed, out_specs=P("batch", "seq", None), check_vma=False
    )
```

profile of v0, /device:TPU:1, one launch (start us, length us, event | category | flops | bytes accessed | tf_op | source)
XLA Modules:
  0.0 1164.6 jit_solution(14377186709707578813)
XLA Ops:
  6.5 2.0 collective-permute-start
  10.2 2.6 collective-permute-start.1
  14.2 6.9 collective-permute-start.2
  24.8 2.9 collective-permute-start.4
  32.2 6.1 convolution_convert_fusion
  46.1 12.6 %slice.229 = bf16[2,256,1152]{1,2,0:T(8,128)(2,1)} reverse(bf16[2,256,1152]{1,2,0:T(8,128)(2,1)S(1)} %copy.148), dimensions={1} | reverse | bytes 2359296 | tf_op jit(solution)/shard_map/slice | solution.py:132
  59.1 3.0 fusion.42
  62.1 18.3 %slice.221 = bf16[2,256,1152]{1,2,0:T(8,128)(2,1)} reverse(bf16[2,256,1152]{1,2,0:T(8,128)(2,1)} %get-tuple-element.343), dimensions={1} | reverse | bytes 2359296 | tf_op jit(solution)/shard_map/slice | solution.py:132
  80.4 18.3 %slice.224 = bf16[2,256,1152]{1,2,0:T(8,128)(2,1)} reverse(bf16[2,256,1152]{1,2,0:T(8,128)(2,1)} %get-tuple-element.345), dimensions={1} | reverse | bytes 2359296 | tf_op jit(solution)/shard_map/slice | solution.py:132
  98.7 12.6 %slice.227 = bf16[2,256,1152]{1,2,0:T(8,128)(2,1)} reverse(bf16[2,256,1152]{1,2,0:T(8,128)(2,1)S(1)} %get-tuple-element.344), dimensions={1} | reverse | bytes 2359296 | tf_op jit(solution)/shard_map/slice | solution.py:132
  111.3 4.1 multiply_convert_fusion
  116.5 2.2 fusion.39
  120.4 4.0 collective-permute-start.5
  125.7 3.6 multiply_convert_fusion.1
  130.7 2.2 fusion.40
  132.9 21.6 %all_gather.32 = bf16[32,1024]{1,0:T(8,128)(2,1)} all-gather(bf16[32,128]{1,0:T(8,128)(2,1)S(1)} %copy-done.21), channel_id=1, replica_groups=mesh['batch'=8,'seq'=32] {'batch'}, dimensions={1}, use_global_device_ids=true | all-gather | bytes 73728 | tf_op jit(solution)/shard_map/all_gather | solution.py:235
  157.8 1.8 bitcast_exponential_fusion
  160.3 110.7 %all-gather.2 = f32[64,1,16]{2,1,0:T(1,128)S(1)} all-gather(f32[2,1,16]{2,1,0:T(1,128)S(1)} %bitcast.220), channel_id=4, replica_groups=mesh['batch'=8,'seq'=32] {'seq'}, dimensions={0}, use_global_device_ids=true | all-gather | bytes 4224 | tf_op jit(solution)/shard_map/all_gather | solution.py:21
  271.0 1.7 copy.129
  275.0 1.8 bitcast_exponential_fusion.1
  277.4 105.7 %all-gather = f32[64,1,16]{2,1,0:T(1,128)S(1)} all-gather(f32[2,1,16]{2,1,0:T(1,128)S(1)} %bitcast.221), channel_id=2, replica_groups=mesh['batch'=8,'seq'=32] {'seq'}, dimensions={0}, use_global_device_ids=true | all-gather | bytes 4224 | tf_op jit(solution)/shard_map/all_gather | solution.py:21
  384.2 2.3 fusion.50
  387.5 3.1 fusion.52
  390.6 1.9 fusion.67
  392.6 165.0 %all-gather.12.cloned.1.call-done = f32[64,16,64,64]{3,2,1,0:T(8,128)} async-done(((f32[2,16,64,64]{3,2,1,0:T(8,128)}), f32[64,16,64,64]{3,2,1,0:T(8,128)}) %all-gather.12.cloned.1.call-update) | async-done | bytes 16777232 | tf_op jit(solution)/shard_map/all_gather | solution.py:21
  557.6 49.2 %while.41 = (s32[]{:T(128)}, f32[2,16,64,64]{3,2,1,0:T(8,128)S(1)}, s32[]{:T(128)}, f32[32,2,16]{2,1,0:T(2,128)S(1)}, f32[32,2,16,64,64]{4,3,2,1,0:T(8,128)}, /*index=5*/s32[]{:T(128)}, s32[]{:T(128)}, s32[]{:T(128)}, s32[]{:T(128)}) while((s32[]{:T(128)}, f32[2,16,64,64]{3,2,1,0:T(8,128)S(1)}, s32[]{:T(128)}, ...), condition=%wide.region_13.14_spmd.clone, body=%wide.region_12.13_spmd.clone.sunk | while | flops 524296 | bytes 1573415 | solution.py:34
  568.2 1.6 fusion.113
  569.8 1.6 fusion.113
  571.4 1.7 fusion.113
  592.9 1.6 fusion.113
  606.7 379.1 %all-gather.10.cloned.1.call-done = f32[64,16,64,64]{3,2,1,0:T(8,128)} async-done(((f32[2,16,64,64]{3,2,1,0:T(8,128)}), f32[64,16,64,64]{3,2,1,0:T(8,128)}) %all-gather.10.cloned.1.call-update) | async-done | bytes 16777232 | tf_op jit(solution)/shard_map/all_gather | solution.py:21
  985.8 48.1 %while.40 = (s32[]{:T(128)}, f32[2,16,64,64]{3,2,1,0:T(8,128)S(1)}, s32[]{:T(128)}, f32[32,2,16]{2,1,0:T(2,128)S(1)}, f32[32,2,16,64,64]{4,3,2,1,0:T(8,128)}, /*index=5*/s32[]{:T(128)}, s32[]{:T(128)}) while((s32[]{:T(128)}, f32[2,16,64,64]{3,2,1,0:T(8,128)S(1)}, s32[]{:T(128)}, f32[32,2,16]{2,1,0:T(2,128)S(1)}, ...), condition=%wide.region_6.7_spmd.clone, body=%wide.region_5.6_spmd.clone.sunk | while | flops 524292 | bytes 1573353 | solution.py:34
  1035.8 7.3 fusion.32
  1043.1 1.8 copy.130
  1044.9 13.7 %rev.20 = f32[2,256,1024]{2,1,0:T(8,128)S(1)} reverse(f32[2,256,1024]{2,1,0:T(8,128)} %copy.130), dimensions={1} | reverse | bytes 4194304 | tf_op jit(solution)/shard_map/jit(_flip)/rev | solution.py:160
  1058.7 2.0 fusion.60
  1060.7 8.7 fusion.27
  1069.4 2.9 copy.119
  1072.3 3.0 multiply_reduce_fusion.1
  1075.4 3.3 add_convert_fusion
  1078.7 3.2 convolution_convert_fusion.1
  1083.2 10.8 collective-permute-done.7
  1094.0 2.8 collective-permute-start.8
  1096.8 9.9 collective-permute-done.8
  1107.1 22.8 %collective-permute-done.9 = bf16[1,256,1024]{2,1,0:T(8,128)(2,1)S(1)} collective-permute-done((bf16[1,256,1024]{2,1,0:T(8,128)(2,1)S(1)}, bf16[1,256,1024]{2,1,0:T(8,128)(2,1)S(1)}, u32[]{:S(2)}, u32[]{:S(2)}) %collective-permute-start.9) | collective-permute-done | bytes 524320 | tf_op jit(solution)/shard_map/ppermute | solution.py:44
  1130.2 12.6 %collective-permute-done.10 = bf16[1,256,1024]{2,1,0:T(8,128)(2,1)S(1)} collective-permute-done((bf16[1,256,1024]{2,1,0:T(8,128)(2,1)S(1)}, bf16[1,256,1024]{2,1,0:T(8,128)(2,1)S(1)}, u32[]{:S(2)}, u32[]{:S(2)}) %collective-permute-start.10) | collective-permute-done | bytes 524320 | tf_op jit(solution)/shard_map/ppermute | solution.py:44
  1142.8 1.5 collective-permute-start.11
  1144.3 12.1 %collective-permute-done.11 = bf16[1,256,1024]{2,1,0:T(8,128)(2,1)S(1)} collective-permute-done((bf16[1,256,1024]{2,1,0:T(8,128)(2,1)S(1)}, bf16[1,256,1024]{2,1,0:T(8,128)(2,1)S(1)}, u32[]{:S(2)}, u32[]{:S(2)}) %collective-permute-start.11) | collective-permute-done | bytes 524320 | tf_op jit(solution)/shard_map/ppermute | solution.py:44
  (283 shorter events, 127.6 us)
Async XLA Ops:
  6.5 33.9 %copy-start = (bf16[1024,16]{0,1:T(8,128)(2,1)S(1)}, bf16[1024,16]{0,1:T(8,128)(2,1)}, u32[]{:S(2)}) copy-start(bf16[1024,16]{0,1:T(8,128)(2,1)} %param.20) | copy-start | bytes 98308
  6.5 551.0 %all-gather.12.cloned.1.call-start = ((), (), s32[]{:S(2)}) async-start(), calls=%async_computation.2 | async-start | bytes 34603008 | tf_op jit(solution)/shard_map/all_gather | solution.py:21
  6.5 3.6 collective-permute-start
  10.2 4.0 collective-permute-start.1
  14.2 7.9 collective-permute-start.2
  22.1 2.7 collective-permute-start.3
  24.8 4.7 collective-permute-start.4
  39.2 19.5 %collective-permute-start.6 = (bf16[2,3,1152]{2,0,1:T(2,128)(2,1)S(1)}, bf16[2,3,1152]{2,0,1:T(2,128)(2,1)S(1)}, u32[]{:S(2)}, u32[]{:S(2)}) collective-permute-start(bf16[2,3,1152]{2,0,1:T(2,128)(2,1)S(1)} %copy.149), channel_id=1, source_target_pairs={{1,0},{2,1},{3,2},{4,3},{5,4},{6,5},{7,6},{8,7},{9,8},{10,9},{11,1... | collective-permute-start | bytes 41480 | tf_op jit(solution)/shard_map/ppermute | solution.py:55
  80.4 30.9 %copy-start.10 = (f32[2,1,1152]{2,0,1:T(2,128)S(1)}, f32[2,1,1152]{2,0,1:T(2,128)}, u32[]{:S(2)}) copy-start(f32[2,1,1152]{2,0,1:T(2,128)} %copy.192) | copy-start | bytes 27652
  80.4 30.9 %copy-start.11 = (f32[2,1,1152]{2,0,1:T(2,128)S(1)}, f32[2,1,1152]{2,0,1:T(2,128)}, u32[]{:S(2)}) copy-start(f32[2,1,1152]{2,0,1:T(2,128)} %copy.193) | copy-start | bytes 27652
  115.4 1.0 copy-start.4
  115.5 3.4 copy-start.17
  115.5 3.4 copy-start.19
  118.7 867.1 %all-gather.10.cloned.1.call-start = ((), (), s32[]{:S(2)}) async-start(), calls=%async_computation.1 | async-start | bytes 34603008 | tf_op jit(solution)/shard_map/all_gather | solution.py:21
  120.4 5.0 collective-permute-start.5
  129.3 1.1 copy-start.3
  129.4 1.3 copy-start.6
  129.4 3.5 copy-start.21
  129.4 25.2 %copy-start.25 = (f32[2,16]{1,0:T(2,128)S(1)}, f32[2,16]{1,0:T(2,128)}, u32[]{:S(2)}) copy-start(f32[2,16]{1,0:T(2,128)} %param.25) | copy-start | bytes 388
  129.5 25.2 %copy-start.22 = (f32[2,1024]{1,0:T(2,128)S(1)}, f32[2,1024]{1,0:T(2,128)}, u32[]{:S(2)}) copy-start(f32[2,1024]{1,0:T(2,128)} %param.26) | copy-start | bytes 24580
  129.5 25.9 %copy-start.18 = (f32[2,16]{1,0:T(2,128)S(1)}, f32[2,16]{1,0:T(2,128)}, u32[]{:S(2)}) copy-start(f32[2,16]{1,0:T(2,128)} %get-tuple-element.378) | copy-start | bytes 388
  129.5 25.9 %copy-start.20 = (f32[2,16]{1,0:T(2,128)S(1)}, f32[2,16]{1,0:T(2,128)}, u32[]{:S(2)}) copy-start(f32[2,16]{1,0:T(2,128)} %get-tuple-element.380) | copy-start | bytes 388
  132.9 945.8 %all-gather.8.cloned.1.call-start = ((), (), s32[]{:S(2)}) async-start(), calls=%async_computation | async-start | bytes 2162688 | tf_op jit(solution)/shard_map/all_gather | solution.py:238
  985.8 49.1 %copy-start.14 = (f32[2,256,16]{1,2,0:T(8,128)S(1)}, f32[2,256,16]{1,2,0:T(8,128)}, u32[]{:S(2)}) copy-start(f32[2,256,16]{1,2,0:T(8,128)} %get-tuple-element.351) | copy-start | bytes 98308
  1033.9 1.2 copy-start.5
  1033.9 1.9 copy-start.9
  1033.9 1.9 copy-start.12
  1033.9 1.9 copy-start.13
  1033.9 1.9 copy-start.24
  1058.6 2.0 copy-start.7
  1058.6 2.0 copy-start.8
  1058.6 2.0 copy-start.15
  1058.6 2.0 copy-start.16
  1058.6 2.0 copy-start.23
  1072.3 3.1 copy-start.2
  1078.7 79.4 %copy-start.1 = (bf16[1024,16]{0,1:T(8,128)(2,1)S(1)}, bf16[1024,16]{0,1:T(8,128)(2,1)}, u32[]{:S(2)}) copy-start(bf16[1024,16]{0,1:T(8,128)(2,1)} %param.20) | copy-start | bytes 98308
  1081.9 12.1 %collective-permute-start.7 = (bf16[1,256,1024]{2,1,0:T(8,128)(2,1)S(1)}, bf16[1,256,1024]{2,1,0:T(8,128)(2,1)S(1)}, u32[]{:S(2)}, u32[]{:S(2)}) collective-permute-start(bf16[1,256,1024]{2,1,0:T(8,128)(2,1)S(1)} %slice_bitcast_fusion), channel_id=1, source_target_pairs={{0,1},{1,0},{2,3},{3,2},{4,5},{5,4},{6,7},{7,6},{8,9},{9,8},{10,11... | collective-permute-start | bytes 1572872 | tf_op jit(solution)/shard_map/ppermute | solution.py:44
  1094.0 12.7 %collective-permute-start.8 = (bf16[1,256,1024]{2,1,0:T(8,128)(2,1)S(1)}, bf16[1,256,1024]{2,1,0:T(8,128)(2,1)S(1)}, u32[]{:S(2)}, u32[]{:S(2)}) collective-permute-start(bf16[1,256,1024]{2,1,0:T(8,128)(2,1)S(1)} %collective-permute-done.7), channel_id=1, source_target_pairs={{0,2},{2,0},{1,3},{3,1},{4,6},{6,4},{5,7},{7,5},{8,10},{10,8},{9,1... | collective-permute-start | bytes 1572872 | tf_op jit(solution)/shard_map/ppermute | solution.py:44
  1106.7 23.1 %collective-permute-start.9 = (bf16[1,256,1024]{2,1,0:T(8,128)(2,1)S(1)}, bf16[1,256,1024]{2,1,0:T(8,128)(2,1)S(1)}, u32[]{:S(2)}, u32[]{:S(2)}) collective-permute-start(bf16[1,256,1024]{2,1,0:T(8,128)(2,1)S(1)} %collective-permute-done.8), channel_id=1, source_target_pairs={{0,4},{4,0},{1,5},{5,1},{2,6},{6,2},{3,7},{7,3},{8,12},{12,8},{9,1... | collective-permute-start | bytes 1572872 | tf_op jit(solution)/shard_map/ppermute | solution.py:44
  1129.8 13.0 %collective-permute-start.10 = (bf16[1,256,1024]{2,1,0:T(8,128)(2,1)S(1)}, bf16[1,256,1024]{2,1,0:T(8,128)(2,1)S(1)}, u32[]{:S(2)}, u32[]{:S(2)}) collective-permute-start(bf16[1,256,1024]{2,1,0:T(8,128)(2,1)S(1)} %collective-permute-done.9), channel_id=1, source_target_pairs={{0,8},{8,0},{1,9},{9,1},{2,10},{10,2},{3,11},{11,3},{4,12},{12,4},... | collective-permute-start | bytes 1572872 | tf_op jit(solution)/shard_map/ppermute | solution.py:44
  1142.8 13.6 %collective-permute-start.11 = (bf16[1,256,1024]{2,1,0:T(8,128)(2,1)S(1)}, bf16[1,256,1024]{2,1,0:T(8,128)(2,1)S(1)}, u32[]{:S(2)}, u32[]{:S(2)}) collective-permute-start(bf16[1,256,1024]{2,1,0:T(8,128)(2,1)S(1)} %collective-permute-done.10), channel_id=1, source_target_pairs={{0,16},{16,0},{1,17},{17,1},{2,18},{18,2},{3,19},{19,3},{4,20},{20... | collective-permute-start | bytes 1572872 | tf_op jit(solution)/shard_map/ppermute | solution.py:44
Sparse Core Ops, SparseCore 0:
  118.8 438.6 all-gather.11
  561.1 424.6 all-gather.9
  989.3 82.1 all-gather.7
where the time goes:
time: 1170 us; the launch traced here: 1160 us
  waiting for transfers between devices  614 us (52%)
  blocking collectives  238 us (20%)
  other arithmetic  123 us (11%)
  local copies, waits for them, and re-layouts  103 us (9%)
  matrix products  42.6 us (4%)
  starting transfers between devices  27.5 us (2%)
  between operations  13.8 us (1%)
    all_gather x2, waiting for transfers between devices, entering_2(): everything = jax.tree.map(lambda part: lax.all_gather(part, axis), value)  544 us
    all_gather x2, blocking collectives, entering_2(): everything = jax.tree.map(lambda part: lax.all_gather(part, axis), value)  216 us
    select_n x64, other arithmetic, hop(): return jax.tree.map(lambda a, b: jnp.where(reached, a, b), new, before)  94.4 us
    ppermute x10, waiting for transfers between devices, from_partner(): return lax.ppermute(block, axis, route)  69.9 us
    slice x4, local copies, waits for them, and re-layouts, direction_pass(): window[:, offset:offset + local_len].astype(jnp.float32)  61.8 us
  transfers between devices with their start and end apart: 15, of which 10 were waited for; matrix products, arithmetic and copies ran while one was open for 17% of the time, Pallas kernels for 0%

commit v1 on v0

v1 whole, which is shorter than its diff:
```python
from functools import partial

import jax
import jax.numpy as jnp
from jax import lax
from jax.experimental import pallas as pl
from jax.experimental.pallas import tpu as pltpu
from jax.sharding import PartitionSpec as P

D = 1024
E = 1024
H = 16
N = 64
CH = 1152
BLOCK = 256
GRAMS = 256
ROWS = 272
LOG2E = 1.4426950408889634
EPS = 1e-05
F32 = jnp.float32
BF16 = jnp.bfloat16
HIGH = lax.Precision.HIGHEST
STRAND = (0, 1, 0, 1)
SET = (0, 1, 1, 0)
RISING = (True, True, False, False)


def iota(shape, dim):
    return lax.broadcasted_iota(jnp.int32, shape, dim)


def silu(x):
    return x * jax.nn.sigmoid(x)


def dot(a, b, **kw):
    return jnp.dot(a, b, preferred_element_type=F32, **kw)


def dot_t(a, b):
    return lax.dot_general(a, b, (((1,), (1,)), ((), ())), preferred_element_type=F32)


def letter_tables(comp, emb_ref, inw_ref, stw_ref, small_refs, gate_hi, gate_lo, conv_in, coef, skip_rows):
    row = iota((16, 1), 0)
    letter = jnp.where(row < 4, row, 4)
    for v in range(4):
        letter = jnp.where(row == 8 + v, comp[v], letter)
    emb = emb_ref[...].astype(F32)
    rows = jnp.zeros((16, D), F32)
    for x in range(4):
        rows = jnp.where(letter == x, emb[x : x + 1], rows)
    rows = rows.astype(BF16)
    projected = dot(rows, inw_ref[...]).astype(BF16).astype(F32)
    gate = silu(projected[:, :E])
    hi = gate.astype(BF16)
    gate_hi[...] = hi
    gate_lo[...] = (gate - hi.astype(F32)).astype(BF16)
    conv_in[...] = projected[:, E:]

    step_raw = dot(rows, stw_ref[...])
    lane = iota((16, 128), 1)
    spread = jnp.where((lane % 16 == iota((16, 128), 0)) & (lane < 64), 1.0, 0.0)
    step_raw = dot(step_raw, spread, precision=HIGH)
    bias_ref, rate_ref, gain_ref = small_refs
    row8 = iota((8, H), 0)
    packed = jnp.zeros((8, H), F32)
    for at, ref in ((0, bias_ref), (2, rate_ref), (4, gain_ref)):
        for d in range(2):
            packed = jnp.where(row8 == at + d, ref[d : d + 1, :], packed)
    spread_small = dot(packed, spread, precision=HIGH)
    sd = iota((1, 128), 1) // 16
    second_set = (sd == 1) | (sd == 2)
    other = sd % 2 == 1
    bias = jnp.where(second_set, spread_small[1:2], spread_small[0:1])
    rate = jnp.where(second_set, spread_small[3:4], spread_small[2:3])
    x = jnp.where(other, step_raw[8:16], step_raw[0:8]) + bias
    step = jnp.maximum(x, 0.0) + jnp.log1p(jnp.exp(-jnp.abs(x)))
    coef[...] = jnp.zeros_like(coef)
    coef[0:8, :] = -rate * step * LOG2E
    coef[8:16, :] = jnp.maximum(jnp.log(step) * LOG2E, -1e30)
    wide = jnp.where(iota((H, E), 1) // 64 == iota((H, E), 0), 1.0, 0.0)
    skip_rows[...] = dot(packed, wide, precision=HIGH)


def gram_tables(edge_letters, conv_in, cw_ref, cb_ref, s01, s23, table):
    letters = conv_in[0:8, :]
    for d in range(2):
        taps = [cw_ref[d, k : k + 1, :] * letters for k in range(4)]
        bias = cb_ref[d : d + 1, :]
        for x in range(4):
            s01[4 * x : 4 * x + 4, :] = bias + taps[0][x : x + 1] + taps[1][0:4]
            s23[4 * x : 4 * x + 4, :] = taps[2][x : x + 1] + taps[3][0:4]
        low = s23[...]
        for i in range(16):
            table[d, 16 * i : 16 * i + 16, :] = silu(s01[i : i + 1, :] + low).astype(BF16)
        total = jnp.broadcast_to(bias, (16, CH))
        for k in (1, 2, 3):
            for x in range(4):
                total = total + jnp.where(edge_letters[d][k] == x, taps[k][x : x + 1], 0.0)
        total = jnp.where(iota((16, 1), 0) < 8, silu(total), 0.0)
        table[d, GRAMS:ROWS, :] = total.astype(BF16)


def shifted(tokens, amount):
    lane = iota(tokens.shape, 1)
    moved = pltpu.roll(tokens, amount % BLOCK, axis=1)
    if amount > 0:
        return jnp.where(lane < amount, pltpu.roll(moved, 1, axis=0), moved)
    return jnp.where(lane >= BLOCK + amount, pltpu.roll(moved, tokens.shape[0] - 1, axis=0), moved)


def mixer(here, comp, tok_ref, emb_ref, inw_ref, stw_ref, cw_ref, cb_ref, small_refs, ng_ref, sc, finish):
    blocks = tok_ref.shape[0]
    letter_tables(
        comp, emb_ref, inw_ref, stw_ref, small_refs, sc["gate_hi"], sc["gate_lo"], sc["conv_in"], sc["coef"], sc["skip_rows"]
    )
    tokens = tok_ref[...]
    others = jnp.zeros_like(tokens)
    for v in range(4):
        others = jnp.where(tokens == v, comp[v], others)

    block_at, lane_at = iota(tokens.shape, 0), iota(tokens.shape, 1)
    low_edge = (block_at == 0) & (lane_at < 3)
    high_edge = (block_at == blocks - 1) & (lane_at >= BLOCK - 3)
    for strand, letters in ((0, tokens), (1, others)):
        rise = 64 * shifted(letters, 3) + 16 * shifted(letters, 2) + 4 * shifted(letters, 1) + letters
        fall = 64 * shifted(letters, -3) + 16 * shifted(letters, -2) + 4 * shifted(letters, -1) + letters
        sc["words"][strand] = jnp.where(low_edge, GRAMS + 4 * strand + lane_at, rise)
        sc["words"][2 + strand] = jnp.where(high_edge, GRAMS + 4 * strand + BLOCK - 1 - lane_at, fall)

    edge_letters = []
    row = iota((16, 1), 0)

    def letter_of(source, block, lane):
        line = source[block : block + 1, :]
        return jnp.sum(jnp.where(iota(line.shape, 1) == lane, line, 0), axis=1, keepdims=True)

    low = [[letter_of(s, 0, j) for j in range(3)] for s in (tokens, others)]
    high = [[letter_of(s, blocks - 1, BLOCK - 1 - j) for j in range(3)] for s in (tokens, others)]
    for d in range(2):
        first, second = (low[0], high[1]) if d == 0 else (high[0], low[1])
        columns = {}
        for k in (1, 2, 3):
            column = jnp.full((16, 1), 4, jnp.int32)
            for strand, letters in ((0, first), (1, second)):
                for j in range(3):
                    at = j - (3 - k)
                    if at >= 0:
                        column = jnp.where(row == 4 * strand + j, letters[at], column)
            columns[k] = column
        edge_letters.append(columns)
    gram_tables(edge_letters, sc["conv_in"], cw_ref, cb_ref, sc["s01"], sc["s23"], sc["table"])

    for v in range(4):
        sc["one_hot"][v * blocks : (v + 1) * blocks, :] = jnp.where(tokens == v, 1.0, 0.0)
    one_hot = sc["one_hot"][...]
    upper = jnp.where(iota((BLOCK, BLOCK), 0) <= iota((BLOCK, BLOCK), 1), 1.0, 0.0)
    inside = dot(one_hot.astype(BF16), upper.astype(BF16))
    sc["inside"][...] = inside
    total = inside[:, BLOCK - 1 : BLOCK]
    rows = 4 * blocks
    a, b = iota((rows, rows), 0), iota((rows, rows), 1)
    aj, bj = a % blocks, b % blocks
    between = (a // blocks == b // blocks) & (((aj < bj) & (bj < here)) | ((here < bj) & (bj < aj)))
    passed = dot(jnp.where(between, 1.0, 0.0).astype(BF16), jnp.broadcast_to(total, inside.shape).astype(BF16))
    before = iota((rows, 1), 0) % blocks < here
    sc["away"][...] = passed + jnp.where(before, total - inside, inside - one_hot)

    coef = sc["coef"][...].T
    column = [coef[:, v : v + 1] for v in range(16)]

    def entry_weights(j, side):
        part = slice(32 * side, 32 * side + 32)
        power = jnp.zeros((32, BLOCK), F32)
        for v in range(4):
            power = power + column[v][part] * sc["away"][pl.ds(v * blocks + j, 1), :]
            power = power + column[8 + v][part] * sc["one_hot"][pl.ds(v * blocks + j, 1), :]
        return jnp.exp2(power).astype(BF16)

    def entering(j, acc, side):
        words = sc["words"][2 * side, pl.ds(j, 1), :]
        hit = jnp.where(iota((GRAMS, BLOCK), 0) == words, 1.0, 0.0).astype(BF16)
        return acc + dot_t(hit, entry_weights(j, side))

    lane = iota((GRAMS, GRAMS), 1)
    other_word = jnp.zeros((1, GRAMS), jnp.int32)
    for place in (64, 16, 4, 1):
        digit = (iota((1, GRAMS), 1) // place) % 4
        for v in range(4):
            other_word = other_word + jnp.where(digit == v, comp[v] * place, 0)
    swap = jnp.where(iota((GRAMS, GRAMS), 0) == other_word, 1.0, 0.0).astype(BF16)
    zero = jnp.zeros((GRAMS, 32), F32)
    for side in (0, 1):
        if side == 0:
            acc = lax.fori_loop(0, here, partial(entering, side=0), zero)
            present = here > 0
            edge_block = 0
        else:
            acc = lax.fori_loop(here + 1, blocks, partial(entering, side=1), zero)
            present = here < blocks - 1
            edge_block = blocks - 1
        acc = acc.astype(BF16)
        swapped = dot(swap, acc)
        lane32 = iota((GRAMS, 32), 1)
        sc["weigh"][side, 0:GRAMS, :] = jnp.where(lane32 < 16, acc.astype(F32), swapped).astype(BF16)
        edge = entry_weights(edge_block, side)
        r16, l16 = iota((16, BLOCK), 0), iota((16, BLOCK), 1)
        pos = l16 if side == 0 else BLOCK - 1 - l16
        pick = jnp.where((pos < 3) & ((r16 == pos) | (r16 == 4 + pos)) & present, 1.0, 0.0).astype(BF16)
        picked = dot_t(pick, edge)
        own = (iota((16, 32), 0) < 4) == (iota((16, 32), 1) < 16)
        sc["weigh"][side, GRAMS:ROWS, :] = jnp.where(own, picked, 0.0).astype(BF16)

    def line(name, v):
        return sc[name][pl.ds(v * blocks + here, 1), :]

    inner = [line("inside", v) for v in range(4)]
    mine = [line("one_hot", v) for v in range(4)]
    sc["run"][...] = jnp.zeros_like(sc["run"])
    for side in (0, 1):
        part = slice(32 * side, 32 * side + 32)
        power = jnp.zeros((32, BLOCK), F32)
        size = jnp.zeros((32, BLOCK), F32)
        for v in range(4):
            count = inner[v] if side == 0 else inner[v][:, BLOCK - 1 : BLOCK] - inner[v] + mine[v]
            power = power + column[v][part] * count
            size = size + column[8 + v][part] * mine[v]
        sc["run"][part, :] = power
        sc["from"][part, :] = power - size
    run = sc["run"][...].T
    for i in range(4):
        sc["local"][i : i + 1, :] = sc["words"][i, pl.ds(here, 1), :].astype(F32)
    sc["local"][4:5, :] = tok_ref[pl.ds(here, 1), :].astype(F32)
    sc["local"][5:128, :] = jnp.zeros((123, BLOCK), F32)
    local = sc["local"][...].T.astype(jnp.int32)
    letter = local[:, 4:5]
    for strand in range(2):
        hit = jnp.where(iota((BLOCK, 16), 1) == letter + 8 * strand, 1.0, 0.0).astype(BF16)
        sc["gate"][strand] = dot(hit, sc["gate_hi"][...]) + dot(hit, sc["gate_lo"][...])

    left = iota((BLOCK, 128), 1) < 64
    half = BLOCK // 2
    t_at, s_at = iota((BLOCK, BLOCK), 0), iota((BLOCK, BLOCK), 1)
    for sd in range(4):
        d, side = SET[sd], sd // 2
        rising = RISING[sd]
        hit = jnp.where(iota((BLOCK, ROWS), 1) == local[:, sd : sd + 1], 1.0, 0.0).astype(BF16)
        conved = dot(hit, sc["table"][d])
        sc["conved"][...] = conved.astype(BF16)
        tail = conved[:, E:]
        b_rows = tail[:, :64].astype(BF16)
        c_rows = pltpu.roll(tail, 64, axis=1)[:, :64].astype(BF16)
        scores = dot_t(c_rows, b_rows)
        reach = s_at <= t_at if rising else s_at >= t_at
        sc["scores"][...] = jnp.where(reach, scores, 0.0)

        place = jnp.where(iota((32, E), 0) == 16 * (sd % 2) + iota((32, E), 1) // 64, 1.0, 0.0).astype(BF16)
        weights = dot(sc["weigh"][side], place)
        weighted = (weights * sc["table"][d, :, 0:E].astype(F32)).astype(BF16)
        b_columns = sc["table"][d, :, E:CH].astype(F32).T.astype(BF16)
        state = dot(b_columns[0:64], weighted).astype(BF16)
        sc["carried"][...] = dot(c_rows, state)

        square = jnp.zeros((BLOCK, 128), F32)
        for pair in range(8):
            cols = slice(128 * pair, 128 * pair + 128)
            values = sc["conved"][:, cols]
            parts, reached = [], []
            for sub in range(2):
                h = 16 * sd + 2 * pair + sub
                to = run[:, h : h + 1]
                source = sc["from"][h : h + 1, :]
                rows_of = []
                for top in (True, False):
                    ts = slice(0, half) if top else slice(half, BLOCK)
                    whole = top != rising
                    ss = slice(0, BLOCK) if whole else ts
                    mixing = jnp.exp2(jnp.minimum(to[ts] - source[:, ss], 100.0)) * sc["scores"][ts, ss]
                    rows_of.append(dot(mixing.astype(BF16), values[ss]))
                parts.append(jnp.concatenate(rows_of, axis=0))
                reached.append(jnp.broadcast_to(to, (BLOCK, 128)))
            both = jnp.where(left, parts[0], parts[1])
            both = both + sc["carried"][:, cols] * jnp.exp2(jnp.where(left, reached[0], reached[1]))
            both = both + sc["skip_rows"][4 + d : 5 + d, cols] * values.astype(F32)
            gated = both * sc["gate"][STRAND[sd], :, cols]
            square = square + gated * gated
            sc["gated"][:, cols] = gated
        mean = jnp.sum(square, axis=1, keepdims=True) * (1.0 / E)
        normed = sc["gated"][...] * lax.rsqrt(mean + EPS) * ng_ref[d : d + 1, :]
        if sd == 0:
            sc["mixed"][...] = normed
        else:
            sc["mixed"][...] += normed
    finish(sc["mixed"][...].astype(BF16))


def scratch(blocks):
    return {
        "gate_hi": pltpu.VMEM((16, E), BF16),
        "gate_lo": pltpu.VMEM((16, E), BF16),
        "conv_in": pltpu.VMEM((16, CH), F32),
        "coef": pltpu.VMEM((128, 128), F32),
        "skip_rows": pltpu.VMEM((8, E), F32),
        "words": pltpu.VMEM((4, blocks, BLOCK), jnp.int32),
        "s01": pltpu.VMEM((16, CH), F32),
        "s23": pltpu.VMEM((16, CH), F32),
        "table": pltpu.VMEM((2, ROWS, CH), BF16),
        "one_hot": pltpu.VMEM((4 * blocks, BLOCK), F32),
        "inside": pltpu.VMEM((4 * blocks, BLOCK), F32),
        "away": pltpu.VMEM((4 * blocks, BLOCK), F32),
        "weigh": pltpu.VMEM((2, ROWS, 32), BF16),
        "run": pltpu.VMEM((128, BLOCK), F32),
        "from": pltpu.VMEM((64, BLOCK), F32),
        "local": pltpu.VMEM((128, BLOCK), F32),
        "gate": pltpu.VMEM((2, BLOCK, E), F32),
        "conved": pltpu.VMEM((BLOCK, CH), BF16),
        "scores": pltpu.VMEM((BLOCK, BLOCK), F32),
        "carried": pltpu.VMEM((BLOCK, E), F32),
        "gated": pltpu.VMEM((BLOCK, E), F32),
        "mixed": pltpu.VMEM((BLOCK, E), F32),
    }


def kernel(names, here_ref, comp_ref, tok, emb, inw, stw, cw, cb, sb, dr, sg, ng, wout, out, *scratch_refs):
    sc = dict(zip(names, scratch_refs))
    comp = [comp_ref[v] for v in range(4)]

    def finish(mixed):
        out[...] = dot(mixed, wout[...]).astype(BF16)

    mixer(here_ref[0], comp, tok, emb, inw, stw, cw, cb, (sb, dr, sg), ng, sc, finish)


def mix(here, comp, tok, emb, inw, stw, cw, cb, sb, dr, sg, ng, wout):
    shapes = scratch(tok.shape[0])
    vmem = pl.BlockSpec(memory_space=pltpu.VMEM)
    smem = pl.BlockSpec(memory_space=pltpu.SMEM)
    return pl.pallas_call(
        partial(kernel, tuple(shapes)),
        out_shape=jax.ShapeDtypeStruct((BLOCK, D), BF16),
        in_specs=[smem, smem] + [vmem] * 11,
        out_specs=vmem,
        scratch_shapes=list(shapes.values()),
        compiler_params=pltpu.CompilerParams(vmem_limit_bytes=60 << 20),
    )(here, comp, tok, emb, inw, stw, cw, cb, sb, dr, sg, ng, wout)


def on_device(tok, comp, emb, inw, stw, cw, cb, sb, dr, sg, ng, wout):
    here = lax.axis_index("seq").astype(jnp.int32).reshape(1)
    tokens = lax.all_gather(tok[0], "seq", axis=0, tiled=False)
    columns = lax.all_gather(wout, "batch", axis=1, tiled=True)
    whole = lax.all_gather(columns, "seq", axis=0, tiled=True)
    return mix(here, comp, tokens, emb, inw, stw, cw, cb, sb, dr, sg, ng, whole)[None]


def solution(mesh):
    placed = (P("batch", "seq"),) + (P(),) * 10 + (P("seq", "batch"),)
    return jax.shard_map(
        on_device, mesh=mesh, in_specs=placed, out_specs=P("batch", "seq", None), check_vma=False
    )
```

time: 1170 us -> 174 us (0.15)
  the two profiles are of different devices: /device:TPU:1 before, /device:TPU:64 now
where the time goes in v1:
time: 174 us
  blocking collectives  135 us (78%)
  Pallas kernels  23.8 us (14%)
  between operations  13.4 us (8%)
  local copies, waits for them, and re-layouts  2.23 us (1%)
    all_gather x1, blocking collectives, on_device(): tokens = lax.all_gather(tok[0], 'seq', axis=0, tiled=False)  122 us
    pallas_call x1, Pallas kernels, mix(): pl.pallas_call(partial(kernel, tuple(shapes)), out_shape=jax.ShapeDtypeSt...  23.8 us
    all_gather x1, blocking collectives, on_device(): columns = lax.all_gather(wout, 'batch', axis=1, tiled=True)  13.3 us
  transfers between devices with their start and end apart: 1, of which 0 were waited for; matrix products, arithmetic and copies ran while one was open for 1% of the time, Pallas kernels for 0%

profile of v1, /device:TPU:64, one launch (start us, length us, event | category | flops | bytes accessed | tf_op | source)
XLA Modules:
  0.0 174.3 jit_solution(11855412563638398574)
XLA Ops:
  6.5 0.0 all-gather.3.cloned.1.call-start
  6.5 13.3 %all_gather.10 = bf16[32,1024]{1,0:T(8,128)(2,1)} all-gather(bf16[32,128]{1,0:T(8,128)(2,1)} %param.23), channel_id=1, replica_groups=mesh['batch'=8,'seq'=32] {'batch'}, dimensions={1}, use_global_device_ids=true | all-gather | bytes 73728 | tf_op jit(solution)/shard_map/all_gather | solution.py:352
  19.8 0.0 all-gather.3.cloned.1.call-update
  19.8 121.6 %all-gather = s32[32,1,256]{2,1,0:T(1,128)S(1)} all-gather(s32[1,1,256]{2,1,0:T(1,128)} %bitcast.7), channel_id=1, replica_groups=mesh['batch'=8,'seq'=32] {'seq'}, dimensions={0}, use_global_device_ids=true | all-gather | bytes 33792 | tf_op jit(solution)/shard_map/all_gather | solution.py:351
  141.4 0.6 copy.17
  142.0 1.6 copy.14.stw
  143.7 0.0 all-gather.3.cloned.1.call-done.wout
  143.7 23.8 %shard_map.118 = bf16[256,1024]{1,0:T(8,128)(2,1)} custom-call(s32[1]{0:T(128)} %bitcast.here_ref, s32[4]{0:T(128)} %comp_ref.1, s32[32,256]{1,0:T(8,128)} %bitcast.6, bf16[4,1024]{1,0:T(4,128)(2,1)} %emb.1, bf16[1024,2176]{1,0:T(8,128)(2,1)} %inw.1, bf16[1024,16]{1,0:T(8,128)(2,1)} %copy.14.stw, f32[2,4,1152]{2,1,0:T(4,128)} %cw.1, f32[2,1152]{1,0:T(2,128)} %cb.1, ...), custom_call_target="tpu_custom_call" | custom-call | tf_op jit(solution)/shard_map/pallas_call | solution.py:339
Async XLA Ops:
  6.5 137.1 %all-gather.3.cloned.1.call-start = ((), (), s32[]{:S(2)}) async-start(), calls=%async_computation | async-start | bytes 2162688 | tf_op jit(solution)/shard_map/all_gather | solution.py:353
Sparse Core Ops, SparseCore 0:
  20.0 92.3 all-gather.2

commit v2 on v1

--- a/solution.py
+++ b/solution.py
@@ -58,7 +58,7 @@
     gate_lo[...] = (gate - hi.astype(F32)).astype(BF16)
     conv_in[...] = projected[:, E:]
 
-    step_raw = dot(rows, stw_ref[...])
+    step_raw = dot_t(rows, stw_ref[...])
     lane = iota((16, 128), 1)
     spread = jnp.where((lane % 16 == iota((16, 128), 0)) & (lane < 64), 1.0, 0.0)
     step_raw = dot(step_raw, spread, precision=HIGH)
@@ -83,7 +83,7 @@
     skip_rows[...] = dot(packed, wide, precision=HIGH)
 
 
-def gram_tables(edge_letters, conv_in, cw_ref, cb_ref, s01, s23, table):
+def gram_tables(conv_in, cw_ref, cb_ref, s01, s23, table):
     letters = conv_in[0:8, :]
     for d in range(2):
         taps = [cw_ref[d, k : k + 1, :] * letters for k in range(4)]
@@ -94,6 +94,13 @@
         low = s23[...]
         for i in range(16):
             table[d, 16 * i : 16 * i + 16, :] = silu(s01[i : i + 1, :] + low).astype(BF16)
+
+
+def edge_tables(edge_letters, conv_in, cw_ref, cb_ref, table):
+    letters = conv_in[0:8, :]
+    for d in range(2):
+        taps = [cw_ref[d, k : k + 1, :] * letters for k in range(4)]
+        bias = cb_ref[d : d + 1, :]
         total = jnp.broadcast_to(bias, (16, CH))
         for k in (1, 2, 3):
             for x in range(4):
@@ -110,12 +117,8 @@
     return jnp.where(lane >= BLOCK + amount, pltpu.roll(moved, tokens.shape[0] - 1, axis=0), moved)
 
 
-def mixer(here, comp, tok_ref, emb_ref, inw_ref, stw_ref, cw_ref, cb_ref, small_refs, ng_ref, sc, finish):
-    blocks = tok_ref.shape[0]
-    letter_tables(
-        comp, emb_ref, inw_ref, stw_ref, small_refs, sc["gate_hi"], sc["gate_lo"], sc["conv_in"], sc["coef"], sc["skip_rows"]
-    )
-    tokens = tok_ref[...]
+def mixer(here, comp, tokens, cw_ref, cb_ref, ng_ref, sc, between_scans):
+    blocks = tokens.shape[0]
     others = jnp.zeros_like(tokens)
     for v in range(4):
         others = jnp.where(tokens == v, comp[v], others)
@@ -150,7 +153,7 @@
                         column = jnp.where(row == 4 * strand + j, letters[at], column)
             columns[k] = column
         edge_letters.append(columns)
-    gram_tables(edge_letters, sc["conv_in"], cw_ref, cb_ref, sc["s01"], sc["s23"], sc["table"])
+    edge_tables(edge_letters, sc["conv_in"], cw_ref, cb_ref, sc["table"])
 
     for v in range(4):
         sc["one_hot"][v * blocks : (v + 1) * blocks, :] = jnp.where(tokens == v, 1.0, 0.0)
@@ -170,47 +173,62 @@
     coef = sc["coef"][...].T
     column = [coef[:, v : v + 1] for v in range(16)]
 
+    for side in (0, 1):
+        for v in range(4):
+            part = slice(32 * side, 32 * side + 32)
+            sc["spread"][side, v] = jnp.broadcast_to(column[v][part], (32, 128))
+            sc["spread"][side, 4 + v] = jnp.broadcast_to(column[8 + v][part], (32, 128))
+
     def entry_weights(j, side):
-        part = slice(32 * side, 32 * side + 32)
-        power = jnp.zeros((32, BLOCK), F32)
-        for v in range(4):
-            power = power + column[v][part] * sc["away"][pl.ds(v * blocks + j, 1), :]
-            power = power + column[8 + v][part] * sc["one_hot"][pl.ds(v * blocks + j, 1), :]
-        return jnp.exp2(power).astype(BF16)
-
-    def entering(j, acc, side):
-        words = sc["words"][2 * side, pl.ds(j, 1), :]
-        hit = jnp.where(iota((GRAMS, BLOCK), 0) == words, 1.0, 0.0).astype(BF16)
-        return acc + dot_t(hit, entry_weights(j, side))
-
-    lane = iota((GRAMS, GRAMS), 1)
+        counts = [sc["away"][pl.ds(v * blocks + j, 1), :] for v in range(4)]
+        letter = [sc["one_hot"][pl.ds(v * blocks + j, 1), :] for v in range(4)]
+        halves = []
+        for lanes in (slice(0, 128), slice(128, 256)):
+            power = jnp.zeros((32, 128), F32)
+            for v in range(4):
+                power = power + sc["spread"][side, v] * counts[v][:, lanes]
+                power = power + sc["spread"][side, 4 + v] * letter[v][:, lanes]
+            halves.append(jnp.exp2(power))
+        return jnp.concatenate(halves, axis=1)
+
+    word_of_row = iota((GRAMS, BLOCK), 0).astype(F32).astype(BF16)
+    group = 8
+
+    def entering(step, acc):
+        hits, powers = [], []
+        for i in range(group):
+            j = step * group + i
+            side = jnp.where(j < here, 0, 1)
+            words = sc["words"][2 * side, pl.ds(j, 1), :].astype(F32).astype(BF16)
+            hits.append(jnp.where(word_of_row == words, jnp.ones((), BF16), jnp.zeros((), BF16)))
+            power = entry_weights(j, side)
+            both = [jnp.where(j < here, power, 0.0), jnp.where(j > here, power, 0.0)]
+            powers.append(jnp.concatenate(both, axis=0).astype(BF16))
+        return acc + dot_t(jnp.concatenate(hits, axis=1), jnp.concatenate(powers, axis=1))
+
     other_word = jnp.zeros((1, GRAMS), jnp.int32)
     for place in (64, 16, 4, 1):
         digit = (iota((1, GRAMS), 1) // place) % 4
         for v in range(4):
             other_word = other_word + jnp.where(digit == v, comp[v] * place, 0)
     swap = jnp.where(iota((GRAMS, GRAMS), 0) == other_word, 1.0, 0.0).astype(BF16)
-    zero = jnp.zeros((GRAMS, 32), F32)
+    acc = lax.fori_loop(0, blocks // group, entering, jnp.zeros((GRAMS, 64), F32)).astype(BF16)
+    swapped = dot(swap, acc)
+    lane64 = iota((GRAMS, 64), 1)
+    sc["weigh"][0:GRAMS, :] = jnp.where(lane64 % 32 < 16, acc.astype(F32), swapped).astype(BF16)
+    edges = []
     for side in (0, 1):
-        if side == 0:
-            acc = lax.fori_loop(0, here, partial(entering, side=0), zero)
-            present = here > 0
-            edge_block = 0
-        else:
-            acc = lax.fori_loop(here + 1, blocks, partial(entering, side=1), zero)
-            present = here < blocks - 1
-            edge_block = blocks - 1
-        acc = acc.astype(BF16)
-        swapped = dot(swap, acc)
-        lane32 = iota((GRAMS, 32), 1)
-        sc["weigh"][side, 0:GRAMS, :] = jnp.where(lane32 < 16, acc.astype(F32), swapped).astype(BF16)
-        edge = entry_weights(edge_block, side)
+        present = here > 0 if side == 0 else here < blocks - 1
+        edge = entry_weights(0 if side == 0 else blocks - 1, side)
+        edges.append(jnp.where(present, edge, 0.0).astype(BF16))
+    own = (iota((16, 32), 0) < 4) == (iota((16, 32), 1) < 16)
+    for side in (0, 1):
         r16, l16 = iota((16, BLOCK), 0), iota((16, BLOCK), 1)
         pos = l16 if side == 0 else BLOCK - 1 - l16
-        pick = jnp.where((pos < 3) & ((r16 == pos) | (r16 == 4 + pos)) & present, 1.0, 0.0).astype(BF16)
-        picked = dot_t(pick, edge)
-        own = (iota((16, 32), 0) < 4) == (iota((16, 32), 1) < 16)
-        sc["weigh"][side, GRAMS:ROWS, :] = jnp.where(own, picked, 0.0).astype(BF16)
+        pick = jnp.where((pos < 3) & ((r16 == pos) | (r16 == 4 + pos)), 1.0, 0.0).astype(BF16)
+        picked = jnp.where(own, dot_t(pick, edges[side]), 0.0)
+        sc["edge"][:, 32 * side : 32 * side + 32] = picked
+    sc["weigh"][GRAMS:ROWS, :] = sc["edge"][...].astype(BF16)
 
     def line(name, v):
         return sc[name][pl.ds(v * blocks + here, 1), :]
@@ -231,7 +249,7 @@
     run = sc["run"][...].T
     for i in range(4):
         sc["local"][i : i + 1, :] = sc["words"][i, pl.ds(here, 1), :].astype(F32)
-    sc["local"][4:5, :] = tok_ref[pl.ds(here, 1), :].astype(F32)
+    sc["local"][4:5, :] = sc["tokens"][pl.ds(here, 1), :].astype(F32)
     sc["local"][5:128, :] = jnp.zeros((123, BLOCK), F32)
     local = sc["local"][...].T.astype(jnp.int32)
     letter = local[:, 4:5]
@@ -255,8 +273,8 @@
         reach = s_at <= t_at if rising else s_at >= t_at
         sc["scores"][...] = jnp.where(reach, scores, 0.0)
 
-        place = jnp.where(iota((32, E), 0) == 16 * (sd % 2) + iota((32, E), 1) // 64, 1.0, 0.0).astype(BF16)
-        weights = dot(sc["weigh"][side], place)
+        place = jnp.where(iota((64, E), 0) == 16 * sd + iota((64, E), 1) // 64, 1.0, 0.0).astype(BF16)
+        weights = dot(sc["weigh"][...], place)
         weighted = (weights * sc["table"][d, :, 0:E].astype(F32)).astype(BF16)
         b_columns = sc["table"][d, :, E:CH].astype(F32).T.astype(BF16)
         state = dot(b_columns[0:64], weighted).astype(BF16)
@@ -292,7 +310,8 @@
             sc["mixed"][...] = normed
         else:
             sc["mixed"][...] += normed
-    finish(sc["mixed"][...].astype(BF16))
+        between_scans(sd)
+    return sc["mixed"][...].astype(BF16)
 
 
 def scratch(blocks):
@@ -309,7 +328,10 @@
         "one_hot": pltpu.VMEM((4 * blocks, BLOCK), F32),
         "inside": pltpu.VMEM((4 * blocks, BLOCK), F32),
         "away": pltpu.VMEM((4 * blocks, BLOCK), F32),
-        "weigh": pltpu.VMEM((2, ROWS, 32), BF16),
+        "weigh": pltpu.VMEM((ROWS, 64), BF16),
+        "edge": pltpu.VMEM((16, 64), F32),
+        "spread": pltpu.VMEM((2, 8, 32, 128), F32),
+        "tokens": pltpu.VMEM((blocks, BLOCK), jnp.int32),
         "run": pltpu.VMEM((128, BLOCK), F32),
         "from": pltpu.VMEM((64, BLOCK), F32),
         "local": pltpu.VMEM((128, BLOCK), F32),
@@ -322,36 +344,157 @@
     }
 
 
-def kernel(names, here_ref, comp_ref, tok, emb, inw, stw, cw, cb, sb, dr, sg, ng, wout, out, *scratch_refs):
-    sc = dict(zip(names, scratch_refs))
+MESH = pl.DeviceIdType.MESH
+PARAMS = 10
+
+
+def kernel(names, *refs):
+    params, shard = refs[:PARAMS], refs[PARAMS]
+    tok, out = refs[PARAMS + 1], refs[PARAMS + 2]
+    sc = dict(zip(names, refs[PARAMS + 3 :]))
+    batch, here = lax.axis_index("batch"), lax.axis_index("seq")
+    z_low, core = lax.div(batch, 2), lax.rem(batch, 2)
+    y, z_high, x = lax.div(here, 8), lax.rem(lax.div(here, 4), 2), lax.rem(here, 4)
+    z, plane = z_high * 4 + z_low, y * 4 + x
+    received, wall = sc["received"], sc["wall"]
+
+    def on_z(other):
+        return (lax.rem(other, 4) * 2 + core, y * 8 + lax.div(other, 4) * 4 + x)
+
+    def on_plane(other):
+        return (batch, lax.div(other, 4) * 8 + z_high * 4 + lax.rem(other, 4))
+
+    partner = (z_low * 2 + 1 - core, here)
+
+    barrier = pltpu.get_barrier_semaphore()
+
+    def greet(device):
+        pl.semaphore_signal(barrier, inc=1, device_id=device, device_id_type=MESH)
+
+    def greet_seq(k, _):
+        greet((batch, lax.rem(here + k, 32)))
+        return 0
+
+    def greet_z(k, _):
+        greet((lax.rem(z_low + k, 4) * 2 + core, y * 8 + x))
+        greet((lax.rem(z_low + k, 4) * 2 + core, y * 8 + 4 + x))
+        return 0
+
+    lax.fori_loop(1, 32, greet_seq, 0)
+    lax.fori_loop(1, 4, greet_z, 0)
+    greet(partner)
+
+    fetch = [
+        pltpu.make_async_copy(tok, received.at[here], sc["own_sem"].at[0]),
+        pltpu.make_async_copy(shard, wall.at[core, plane, z], sc["own_sem"].at[1]),
+    ]
+    held = []
+    for i, ref in enumerate(params):
+        held.append(sc[f"held{i}"])
+        fetch.append(pltpu.make_async_copy(ref, held[i], sc["own_sem"].at[2 + i]))
+    for copy in fetch:
+        copy.start()
+    for copy in fetch:
+        copy.wait()
+    comp_ref, emb, inw, stw, cw, cb, sb, dr, sg, ng = held[:10]
     comp = [comp_ref[v] for v in range(4)]
-
-    def finish(mixed):
-        out[...] = dot(mixed, wout[...]).astype(BF16)
-
-    mixer(here_ref[0], comp, tok, emb, inw, stw, cw, cb, (sb, dr, sg), ng, sc, finish)
-
-
-def mix(here, comp, tok, emb, inw, stw, cw, cb, sb, dr, sg, ng, wout):
-    shapes = scratch(tok.shape[0])
-    vmem = pl.BlockSpec(memory_space=pltpu.VMEM)
-    smem = pl.BlockSpec(memory_space=pltpu.SMEM)
-    return pl.pallas_call(
+    letter_tables(
+        comp, emb, inw, stw, (sb, dr, sg), sc["gate_hi"], sc["gate_lo"], sc["conv_in"], sc["coef"], sc["skip_rows"]
+    )
+    gram_tables(sc["conv_in"], cw, cb, sc["s01"], sc["s23"], sc["table"])
+    pl.semaphore_wait(barrier, 38)
+
+    def token_copy(k, owner, device):
+        return pltpu.make_async_remote_copy(
+            received.at[owner], received.at[owner], sc["token_send"].at[k], sc["token_recv"].at[owner], device, MESH
+        )
+
+    def z_copy(k, owner, device):
+        piece = wall.at[core, plane, owner]
+        return pltpu.make_async_remote_copy(piece, piece, sc["z_send"].at[k], sc["z_recv"].at[owner], device, MESH)
+
+    def plane_copy(k, owner, device):
+        piece = wall.at[core, owner]
+        return pltpu.make_async_remote_copy(
+            piece, piece, sc["plane_send"].at[k], sc["plane_recv"].at[owner], device, MESH
+        )
+
+    def core_copy(side, owner):
+        piece = wall.at[side, owner]
+        return pltpu.make_async_remote_copy(
+            piece, piece, sc["core_send"].at[owner], sc["core_recv"].at[owner], partner, MESH
+        )
+
+    def each(count, act):
+        def go(k, _):
+            act(k)
+            return 0
+
+        lax.fori_loop(1, count, go, 0)
+
+    def seq_peer(k):
+        return lax.rem(here + k, 32)
+
+    def z_peer(k):
+        return lax.rem(z + k, 8)
+
+    def plane_peer(k):
+        return lax.rem(plane + k, 16)
+
+    each(8, lambda k: z_copy(k, z, on_z(z_peer(k))).start())
+    each(32, lambda k: token_copy(k, here, (batch, seq_peer(k))).start())
+    each(8, lambda k: z_copy(k, z_peer(k), on_z(z_peer(k))).wait_recv())
+    each(16, lambda k: plane_copy(k, plane, on_plane(plane_peer(k))).start())
+    core_copy(core, plane).start()
+    each(32, lambda k: token_copy(k, seq_peer(k), (batch, seq_peer(k))).wait_recv())
+    for j in range(32):
+        sc["tokens"][j : j + 1, :] = received[j]
+
+    def between_scans(sd):
+        if sd == 2:
+            def pass_on(k):
+                plane_copy(k, plane_peer(k), on_plane(plane_peer(k))).wait_recv()
+                core_copy(core, plane_peer(k)).start()
+
+            each(16, pass_on)
+
+    mixed = mixer(here, comp, sc["tokens"][...], cw, cb, ng, sc, between_scans)
+    lax.fori_loop(0, 16, lambda q, c: (core_copy(1 - core, q).wait_recv(), c)[1], 0)
+    order = [(4 * (s // 8) + s % 4, 4 * ((s // 4) % 2)) for s in range(32)]
+    for low in range(4):
+        sides = [jnp.concatenate([wall[c, p, h + low] for p, h in order], axis=0) for c in range(2)]
+        out[:, 256 * low : 256 * low + 256] = dot(mixed, jnp.concatenate(sides, axis=1)).astype(BF16)
+
+    each(8, lambda k: z_copy(k, z, on_z(z_peer(k))).wait_send())
+    each(32, lambda k: token_copy(k, here, (batch, seq_peer(k))).wait_send())
+    each(16, lambda k: plane_copy(k, plane, on_plane(plane_peer(k))).wait_send())
+    lax.fori_loop(0, 16, lambda q, c: (core_copy(core, q).wait_send(), c)[1], 0)
+
+
+def on_device(tok, comp, emb, inw, stw, cw, cb, sb, dr, sg, ng, wout):
+    params = [comp, emb, inw, stw.T, cw, cb, sb, dr, sg, ng]
+    shapes = scratch(32)
+    shapes["received"] = pltpu.VMEM((32, 1, BLOCK), jnp.int32)
+    shapes["wall"] = pltpu.VMEM((2, 16, 8, 32, 128), BF16)
+    shapes["own_sem"] = pltpu.SemaphoreType.DMA((2 + PARAMS,))
+    for name, count in (("token", 32), ("z", 8), ("plane", 16), ("core", 16)):
+        shapes[name + "_send"] = pltpu.SemaphoreType.DMA((count,))
+        shapes[name + "_recv"] = pltpu.SemaphoreType.DMA((count,))
+    for i, value in enumerate(params):
+        space = pltpu.SMEM if value.ndim == 1 else pltpu.VMEM
+        shapes[f"held{i}"] = space(value.shape, value.dtype)
+    anywhere = pl.BlockSpec(memory_space=pl.ANY)
+    out = pl.pallas_call(
         partial(kernel, tuple(shapes)),
         out_shape=jax.ShapeDtypeStruct((BLOCK, D), BF16),
-        in_specs=[smem, smem] + [vmem] * 11,
-        out_specs=vmem,
+        in_specs=[anywhere] * (PARAMS + 2),
+        out_specs=pl.BlockSpec(memory_space=pltpu.VMEM),
         scratch_shapes=list(shapes.values()),
-        compiler_params=pltpu.CompilerParams(vmem_limit_bytes=60 << 20),
-    )(here, comp, tok, emb, inw, stw, cw, cb, sb, dr, sg, ng, wout)
-
-
-def on_device(tok, comp, emb, inw, stw, cw, cb, sb, dr, sg, ng, wout):
-    here = lax.axis_index("seq").astype(jnp.int32).reshape(1)
-    tokens = lax.all_gather(tok[0], "seq", axis=0, tiled=False)
-    columns = lax.all_gather(wout, "batch", axis=1, tiled=True)
-    whole = lax.all_gather(columns, "seq", axis=0, tiled=True)
-    return mix(here, comp, tokens, emb, inw, stw, cw, cb, sb, dr, sg, ng, whole)[None]
+        compiler_params=pltpu.CompilerParams(
+            collective_id=0, has_side_effects=True, vmem_limit_bytes=60 << 20
+        ),
+    )(*params, wout, tok)
+    return out[None]
 
 
 def solution(mesh):

time: 174 us -> 38 us (0.22)
  the two profiles are of different devices: /device:TPU:64 before, /device:TPU:1 now
where the time goes in v2:
time: 38 us; the launch traced here: 37.9 us
  Pallas kernels  36 us (95%)
  local copies, waits for them, and re-layouts  1.87 us (5%)
    pallas_call x1, Pallas kernels, on_device(): pl.pallas_call(partial(kernel, tuple(shapes)), out_shape=jax.ShapeDtypeSt...  36 us
    unnamed x1, local copies, waits for them, and re-layouts  1.87 us

profile of v2, /device:TPU:1, one launch (start us, length us, event | category | flops | bytes accessed | tf_op | source)
XLA Modules:
  0.0 37.9 jit_solution(3857040789160581653)
XLA Ops:
  0.0 36.0 %shard_map.118 = bf16[256,1024]{1,0:T(8,128)(2,1)} custom-call(s32[4]{0:T(128)} %refs_0_.1, bf16[4,1024]{1,0:T(4,128)(2,1)} %refs_1_.1, bf16[1024,2176]{1,0:T(8,128)(2,1)} %refs_2_.1, bf16[16,1024]{1,0:T(8,128)(2,1)} %bitcast.3, f32[2,4,1152]{2,1,0:T(4,128)} %refs_4_.1, f32[2,1152]{1,0:T(2,128)} %refs_5_.1, f32[2,16]{1,0:T(2,128)} %refs_6_.1, ...), custom_call_target="tpu_custom_call" | custom-call | tf_op jit(solution)/shard_map/pallas_call | solution.py:487
  36.0 1.9 %copy.14 = bf16[1,256,1024]{2,1,0:T(8,128)(2,1)} copy(bf16[1,256,1024]{2,1,0:T(8,128)(2,1)} %bitcast.2) | data formatting | bytes 1048576

commit v3 on v2

--- a/solution.py
+++ b/solution.py
@@ -41,7 +41,7 @@
     return lax.dot_general(a, b, (((1,), (1,)), ((), ())), preferred_element_type=F32)
 
 
-def letter_tables(comp, emb_ref, inw_ref, stw_ref, small_refs, gate_hi, gate_lo, conv_in, coef, skip_rows):
+def letter_tables(comp, emb_ref, inw_ref, stw_ref, small_refs, gate_parts, conv_in, coef, skip_rows):
     row = iota((16, 1), 0)
     letter = jnp.where(row < 4, row, 4)
     for v in range(4):
@@ -54,8 +54,8 @@
     projected = dot(rows, inw_ref[...]).astype(BF16).astype(F32)
     gate = silu(projected[:, :E])
     hi = gate.astype(BF16)
-    gate_hi[...] = hi
-    gate_lo[...] = (gate - hi.astype(F32)).astype(BF16)
+    gate_parts[0:16, :] = hi
+    gate_parts[16:32, :] = (gate - hi.astype(F32)).astype(BF16)
     conv_in[...] = projected[:, E:]
 
     step_raw = dot_t(rows, stw_ref[...])
@@ -117,7 +117,63 @@
     return jnp.where(lane >= BLOCK + amount, pltpu.roll(moved, tokens.shape[0] - 1, axis=0), moved)
 
 
-def mixer(here, comp, tokens, cw_ref, cb_ref, ng_ref, sc, between_scans):
+def local_counts(mine, sc):
+    hot = jnp.concatenate([jnp.where(mine == v, 1.0, 0.0) for v in range(4)] + [jnp.zeros((4, BLOCK), F32)], axis=0)
+    upper = jnp.where(iota((BLOCK, BLOCK), 0) <= iota((BLOCK, BLOCK), 1), 1.0, 0.0)
+    count = dot(hot.astype(BF16), upper.astype(BF16))
+    coef = sc["coef"][...].T
+    sc["run"][...] = jnp.zeros_like(sc["run"])
+    for side in (0, 1):
+        part = slice(32 * side, 32 * side + 32)
+        power = jnp.zeros((32, BLOCK), F32)
+        size = jnp.zeros((32, BLOCK), F32)
+        for v in range(4):
+            passed = count[v : v + 1]
+            if side == 1:
+                passed = passed[:, BLOCK - 1 : BLOCK] - passed + hot[v : v + 1]
+            power = power + coef[part, v : v + 1] * passed
+            size = size + coef[part, 8 + v : 9 + v] * hot[v : v + 1]
+        sc["run"][part, :] = power
+        sc["from"][part, :] = power - size
+        for v in range(8):
+            at = v if v < 4 else v + 4
+            sc["spread"][side, v] = jnp.broadcast_to(coef[part, at : at + 1], (32, 128))
+    sc["run_t"][...] = sc["run"][...].T
+    letter = jnp.broadcast_to(mine.astype(F32), (128, BLOCK)).T.astype(jnp.int32)[:, 0:32]
+    for strand in range(2):
+        hit = jnp.where(iota((BLOCK, 32), 1) % 16 == letter + 8 * strand, 1.0, 0.0).astype(BF16)
+        sc["gate"][strand] = dot(hit, sc["gate_parts"][...])
+    for d in range(2):
+        sc["b_columns"][d, :, 0:GRAMS] = sc["table"][d, 0:GRAMS, E:CH].astype(F32).T.astype(BF16)
+
+
+def local_decays(sd, sc):
+    left = iota((BLOCK, 128), 1) < 64
+    half = BLOCK // 2
+    rising = RISING[sd]
+    t_at, s_at = iota((half, half), 0), iota((half, half), 1)
+    reach = s_at <= t_at if rising else s_at >= t_at
+    for pair in range(8):
+        reached = []
+        for sub in range(2):
+            h = 16 * sd + 2 * pair + sub
+            to = jnp.broadcast_to(sc["run_t"][:, h : h + 1], (BLOCK, 128))
+            reached.append(to)
+            source = sc["from"][h : h + 1, :]
+            for top in (0, 1):
+                for side in (0, 1):
+                    ts, ss = slice(half * top, half * top + half), slice(half * side, half * side + half)
+                    if top == side:
+                        decay = jnp.where(reach, jnp.exp2(to[ts] - source[:, ss]), 0.0)
+                    elif (side < top) == rising:
+                        decay = jnp.exp2(to[ts] - source[:, ss])
+                    else:
+                        continue
+                    sc["decay"][h, ts, ss] = decay.astype(BF16)
+        sc["grow"][sd, :, 128 * pair : 128 * pair + 128] = jnp.exp2(jnp.where(left, reached[0], reached[1]))
+
+
+def mixer(here, comp, tokens, cw_ref, cb_ref, ng_ref, sc, after_history, between_scans):
     blocks = tokens.shape[0]
     others = jnp.zeros_like(tokens)
     for v in range(4):
@@ -169,15 +225,6 @@
     passed = dot(jnp.where(between, 1.0, 0.0).astype(BF16), jnp.broadcast_to(total, inside.shape).astype(BF16))
     before = iota((rows, 1), 0) % blocks < here
     sc["away"][...] = passed + jnp.where(before, total - inside, inside - one_hot)
-
-    coef = sc["coef"][...].T
-    column = [coef[:, v : v + 1] for v in range(16)]
-
-    for side in (0, 1):
-        for v in range(4):
-            part = slice(32 * side, 32 * side + 32)
-            sc["spread"][side, v] = jnp.broadcast_to(column[v][part], (32, 128))
-            sc["spread"][side, 4 + v] = jnp.broadcast_to(column[8 + v][part], (32, 128))
 
     def entry_weights(j, side):
         counts = [sc["away"][pl.ds(v * blocks + j, 1), :] for v in range(4)]
@@ -230,76 +277,49 @@
         sc["edge"][:, 32 * side : 32 * side + 32] = picked
     sc["weigh"][GRAMS:ROWS, :] = sc["edge"][...].astype(BF16)
 
-    def line(name, v):
-        return sc[name][pl.ds(v * blocks + here, 1), :]
-
-    inner = [line("inside", v) for v in range(4)]
-    mine = [line("one_hot", v) for v in range(4)]
-    sc["run"][...] = jnp.zeros_like(sc["run"])
-    for side in (0, 1):
-        part = slice(32 * side, 32 * side + 32)
-        power = jnp.zeros((32, BLOCK), F32)
-        size = jnp.zeros((32, BLOCK), F32)
-        for v in range(4):
-            count = inner[v] if side == 0 else inner[v][:, BLOCK - 1 : BLOCK] - inner[v] + mine[v]
-            power = power + column[v][part] * count
-            size = size + column[8 + v][part] * mine[v]
-        sc["run"][part, :] = power
-        sc["from"][part, :] = power - size
-    run = sc["run"][...].T
     for i in range(4):
         sc["local"][i : i + 1, :] = sc["words"][i, pl.ds(here, 1), :].astype(F32)
-    sc["local"][4:5, :] = sc["tokens"][pl.ds(here, 1), :].astype(F32)
-    sc["local"][5:128, :] = jnp.zeros((123, BLOCK), F32)
+    sc["local"][4:128, :] = jnp.zeros((124, BLOCK), F32)
     local = sc["local"][...].T.astype(jnp.int32)
-    letter = local[:, 4:5]
-    for strand in range(2):
-        hit = jnp.where(iota((BLOCK, 16), 1) == letter + 8 * strand, 1.0, 0.0).astype(BF16)
-        sc["gate"][strand] = dot(hit, sc["gate_hi"][...]) + dot(hit, sc["gate_lo"][...])
-
+    for d in range(2):
+        tail = sc["table"][d, GRAMS:ROWS, E:CH].astype(F32)
+        tail = jnp.concatenate([tail, jnp.zeros((112, CH - E), F32)], axis=0).T
+        sc["b_columns"][d, :, GRAMS:ROWS] = tail[:, 0 : ROWS - GRAMS].astype(BF16)
+
+    after_history()
     left = iota((BLOCK, 128), 1) < 64
     half = BLOCK // 2
-    t_at, s_at = iota((BLOCK, BLOCK), 0), iota((BLOCK, BLOCK), 1)
     for sd in range(4):
-        d, side = SET[sd], sd // 2
-        rising = RISING[sd]
+        d, rising = SET[sd], RISING[sd]
         hit = jnp.where(iota((BLOCK, ROWS), 1) == local[:, sd : sd + 1], 1.0, 0.0).astype(BF16)
         conved = dot(hit, sc["table"][d])
         sc["conved"][...] = conved.astype(BF16)
         tail = conved[:, E:]
         b_rows = tail[:, :64].astype(BF16)
         c_rows = pltpu.roll(tail, 64, axis=1)[:, :64].astype(BF16)
-        scores = dot_t(c_rows, b_rows)
-        reach = s_at <= t_at if rising else s_at >= t_at
-        sc["scores"][...] = jnp.where(reach, scores, 0.0)
+        sc["scores"][...] = dot_t(c_rows, b_rows).astype(BF16)
 
         place = jnp.where(iota((64, E), 0) == 16 * sd + iota((64, E), 1) // 64, 1.0, 0.0).astype(BF16)
         weights = dot(sc["weigh"][...], place)
-        weighted = (weights * sc["table"][d, :, 0:E].astype(F32)).astype(BF16)
-        b_columns = sc["table"][d, :, E:CH].astype(F32).T.astype(BF16)
-        state = dot(b_columns[0:64], weighted).astype(BF16)
+        weighted = weights.astype(BF16) * sc["table"][d, :, 0:E]
+        state = dot(sc["b_columns"][d, 0:64, :], weighted).astype(BF16)
         sc["carried"][...] = dot(c_rows, state)
 
         square = jnp.zeros((BLOCK, 128), F32)
         for pair in range(8):
             cols = slice(128 * pair, 128 * pair + 128)
             values = sc["conved"][:, cols]
-            parts, reached = [], []
+            parts = []
             for sub in range(2):
                 h = 16 * sd + 2 * pair + sub
-                to = run[:, h : h + 1]
-                source = sc["from"][h : h + 1, :]
                 rows_of = []
                 for top in (True, False):
                     ts = slice(0, half) if top else slice(half, BLOCK)
-                    whole = top != rising
-                    ss = slice(0, BLOCK) if whole else ts
-                    mixing = jnp.exp2(jnp.minimum(to[ts] - source[:, ss], 100.0)) * sc["scores"][ts, ss]
-                    rows_of.append(dot(mixing.astype(BF16), values[ss]))
+                    ss = slice(0, BLOCK) if top != rising else ts
+                    rows_of.append(dot(sc["decay"][h, ts, ss] * sc["scores"][ts, ss], values[ss]))
                 parts.append(jnp.concatenate(rows_of, axis=0))
-                reached.append(jnp.broadcast_to(to, (BLOCK, 128)))
             both = jnp.where(left, parts[0], parts[1])
-            both = both + sc["carried"][:, cols] * jnp.exp2(jnp.where(left, reached[0], reached[1]))
+            both = both + sc["carried"][:, cols] * sc["grow"][sd, :, cols]
             both = both + sc["skip_rows"][4 + d : 5 + d, cols] * values.astype(F32)
             gated = both * sc["gate"][STRAND[sd], :, cols]
             square = square + gated * gated
@@ -316,8 +336,7 @@
 
 def scratch(blocks):
     return {
-        "gate_hi": pltpu.VMEM((16, E), BF16),
-        "gate_lo": pltpu.VMEM((16, E), BF16),
+        "gate_parts": pltpu.VMEM((32, E), BF16),
         "conv_in": pltpu.VMEM((16, CH), F32),
         "coef": pltpu.VMEM((128, 128), F32),
         "skip_rows": pltpu.VMEM((8, E), F32),
@@ -337,7 +356,11 @@
         "local": pltpu.VMEM((128, BLOCK), F32),
         "gate": pltpu.VMEM((2, BLOCK, E), F32),
         "conved": pltpu.VMEM((BLOCK, CH), BF16),
-        "scores": pltpu.VMEM((BLOCK, BLOCK), F32),
+        "scores": pltpu.VMEM((BLOCK, BLOCK), BF16),
+        "run_t": pltpu.VMEM((BLOCK, 128), F32),
+        "b_columns": pltpu.VMEM((2, 128, ROWS), BF16),
+        "decay": pltpu.VMEM((64, BLOCK, BLOCK), BF16),
+        "grow": pltpu.VMEM((4, BLOCK, E), F32),
         "carried": pltpu.VMEM((BLOCK, E), F32),
         "gated": pltpu.VMEM((BLOCK, E), F32),
         "mixed": pltpu.VMEM((BLOCK, E), F32),
@@ -355,131 +378,161 @@
     batch, here = lax.axis_index("batch"), lax.axis_index("seq")
     z_low, core = lax.div(batch, 2), lax.rem(batch, 2)
     y, z_high, x = lax.div(here, 8), lax.rem(lax.div(here, 4), 2), lax.rem(here, 4)
-    z, plane = z_high * 4 + z_low, y * 4 + x
+    z = z_high * 4 + z_low
     received, wall = sc["received"], sc["wall"]
-
-    def on_z(other):
-        return (lax.rem(other, 4) * 2 + core, y * 8 + lax.div(other, 4) * 4 + x)
-
-    def on_plane(other):
-        return (batch, lax.div(other, 4) * 8 + z_high * 4 + lax.rem(other, 4))
-
     partner = (z_low * 2 + 1 - core, here)
-
     barrier = pltpu.get_barrier_semaphore()
 
     def greet(device):
         pl.semaphore_signal(barrier, inc=1, device_id=device, device_id_type=MESH)
 
-    def greet_seq(k, _):
-        greet((batch, lax.rem(here + k, 32)))
-        return 0
-
-    def greet_z(k, _):
+    def at(xx, yy, zz):
+        return (lax.rem(zz, 4) * 2 + core, yy * 8 + lax.div(zz, 4) * 4 + xx)
+
+    def loop(first, last, act):
+        def go(k, carry):
+            act(k)
+            return carry
+
+        lax.fori_loop(first, last, go, 0)
+
+    def greet_z(k):
         greet((lax.rem(z_low + k, 4) * 2 + core, y * 8 + x))
         greet((lax.rem(z_low + k, 4) * 2 + core, y * 8 + 4 + x))
-        return 0
-
-    lax.fori_loop(1, 32, greet_seq, 0)
-    lax.fori_loop(1, 4, greet_z, 0)
+
+    loop(1, 32, lambda k: greet((batch, lax.rem(here + k, 32))))
+    loop(1, 4, greet_z)
     greet(partner)
 
-    fetch = [
-        pltpu.make_async_copy(tok, received.at[here], sc["own_sem"].at[0]),
-        pltpu.make_async_copy(shard, wall.at[core, plane, z], sc["own_sem"].at[1]),
-    ]
-    held = []
+    def copy_of(piece, send, recv, device):
+        return pltpu.make_async_remote_copy(piece, piece, send, recv, device, MESH)
+
+    def seq_peer(k):
+        return lax.rem(here + k, 32)
+
+    def token_copy(k, owner):
+        return copy_of(received.at[owner], sc["token_send"].at[k], sc["token_recv"].at[owner], (batch, seq_peer(k)))
+
+    mine, inner, outer = [y * 4 + x, x * 4 + y], [x, y], [y, x]
+
+    def z_copy(c, k, owner):
+        piece = wall.at[core, c, mine[c], owner]
+        return copy_of(piece, sc["z_send"].at[c, k], sc["z_recv"].at[c, owner], at(x, y, lax.rem(z + k, 8)))
+
+    def along(c, k, first):
+        step_x, step_y = at(lax.rem(x + k, 4), y, z), at(x, lax.rem(y + k, 4), z)
+        return step_x if (c == 0) == first else step_y
+
+    def second_copy(c, k, owner):
+        piece = wall.at[core, c, 4 * outer[c] + owner]
+        return copy_of(piece, sc["second_send"].at[c, k], sc["second_recv"].at[c, owner], along(c, k, True))
+
+    def third_copy(c, k, owner):
+        piece = wall.at[core, c, pl.ds(4 * owner, 4)]
+        return copy_of(piece, sc["third_send"].at[c, k], sc["third_recv"].at[c, owner], along(c, k, False))
+
+    def core_copy(side, c, owner):
+        piece = wall.at[side, c, pl.ds(4 * owner, 4)]
+        return copy_of(piece, sc["core_send"].at[c, owner], sc["core_recv"].at[c, owner], partner)
+
+    first = [pltpu.make_async_copy(tok, received.at[here], sc["own_sem"].at[0])]
+    for c in range(2):
+        half = shard.at[16 * c : 16 * c + 16]
+        first.append(pltpu.make_async_copy(half, wall.at[core, c, mine[c], z], sc["own_sem"].at[1 + c]))
+    fetch, held = [], []
     for i, ref in enumerate(params):
         held.append(sc[f"held{i}"])
-        fetch.append(pltpu.make_async_copy(ref, held[i], sc["own_sem"].at[2 + i]))
-    for copy in fetch:
+        fetch.append(pltpu.make_async_copy(ref, held[i], sc["own_sem"].at[3 + i]))
+    for copy in first + fetch:
         copy.start()
+    for copy in first:
+        copy.wait()
+
+    def send():
+        pl.semaphore_wait(barrier, 38)
+        for c in range(2):
+            loop(1, 8, lambda k: z_copy(c, k, z).start())
+        loop(1, 32, lambda k: token_copy(k, here).start())
+
+    def pass_on_z():
+        for c in range(2):
+            loop(1, 8, lambda k: z_copy(c, k, lax.rem(z + k, 8)).wait_recv())
+            loop(1, 4, lambda k: second_copy(c, k, inner[c]).start())
+
+    distance = z + lax.min(y, 4 - y) + lax.min(x, 4 - x)
+    soon = (z_high == 0) & (distance < 4)
+    later = (z_high == 0) & (distance >= 4)
+    last = z_high == 1
+
+    pl.when(last)(send)
     for copy in fetch:
         copy.wait()
-    comp_ref, emb, inw, stw, cw, cb, sb, dr, sg, ng = held[:10]
+    comp_ref, emb, inw, stw, cw, cb, sb, dr, sg, ng = held
     comp = [comp_ref[v] for v in range(4)]
     letter_tables(
-        comp, emb, inw, stw, (sb, dr, sg), sc["gate_hi"], sc["gate_lo"], sc["conv_in"], sc["coef"], sc["skip_rows"]
+        comp, emb, inw, stw, (sb, dr, sg), sc["gate_parts"], sc["conv_in"], sc["coef"], sc["skip_rows"]
     )
     gram_tables(sc["conv_in"], cw, cb, sc["s01"], sc["s23"], sc["table"])
-    pl.semaphore_wait(barrier, 38)
-
-    def token_copy(k, owner, device):
-        return pltpu.make_async_remote_copy(
-            received.at[owner], received.at[owner], sc["token_send"].at[k], sc["token_recv"].at[owner], device, MESH
-        )
-
-    def z_copy(k, owner, device):
-        piece = wall.at[core, plane, owner]
-        return pltpu.make_async_remote_copy(piece, piece, sc["z_send"].at[k], sc["z_recv"].at[owner], device, MESH)
-
-    def plane_copy(k, owner, device):
-        piece = wall.at[core, owner]
-        return pltpu.make_async_remote_copy(
-            piece, piece, sc["plane_send"].at[k], sc["plane_recv"].at[owner], device, MESH
-        )
-
-    def core_copy(side, owner):
-        piece = wall.at[side, owner]
-        return pltpu.make_async_remote_copy(
-            piece, piece, sc["core_send"].at[owner], sc["core_recv"].at[owner], partner, MESH
-        )
-
-    def each(count, act):
-        def go(k, _):
-            act(k)
-            return 0
-
-        lax.fori_loop(1, count, go, 0)
-
-    def seq_peer(k):
-        return lax.rem(here + k, 32)
-
-    def z_peer(k):
-        return lax.rem(z + k, 8)
-
-    def plane_peer(k):
-        return lax.rem(plane + k, 16)
-
-    each(8, lambda k: z_copy(k, z, on_z(z_peer(k))).start())
-    each(32, lambda k: token_copy(k, here, (batch, seq_peer(k))).start())
-    each(8, lambda k: z_copy(k, z_peer(k), on_z(z_peer(k))).wait_recv())
-    each(16, lambda k: plane_copy(k, plane, on_plane(plane_peer(k))).start())
-    core_copy(core, plane).start()
-    each(32, lambda k: token_copy(k, seq_peer(k), (batch, seq_peer(k))).wait_recv())
+    pl.when(later)(send)
+    local_counts(received[here], sc)
+    pl.when(last)(pass_on_z)
+    local_decays(0, sc)
+    local_decays(1, sc)
+    pl.when(later)(pass_on_z)
+    local_decays(2, sc)
+    local_decays(3, sc)
+
+    @pl.when(soon)
+    def _():
+        send()
+        pass_on_z()
+
+    loop(1, 32, lambda k: token_copy(k, seq_peer(k)).wait_recv())
     for j in range(32):
         sc["tokens"][j : j + 1, :] = received[j]
 
-    def between_scans(sd):
-        if sd == 2:
-            def pass_on(k):
-                plane_copy(k, plane_peer(k), on_plane(plane_peer(k))).wait_recv()
-                core_copy(core, plane_peer(k)).start()
-
-            each(16, pass_on)
-
-    mixed = mixer(here, comp, sc["tokens"][...], cw, cb, ng, sc, between_scans)
-    lax.fori_loop(0, 16, lambda q, c: (core_copy(1 - core, q).wait_recv(), c)[1], 0)
-    order = [(4 * (s // 8) + s % 4, 4 * ((s // 4) % 2)) for s in range(32)]
+    def pass_on_second():
+        for c in range(2):
+            loop(1, 4, lambda k: second_copy(c, k, lax.rem(inner[c] + k, 4)).wait_recv())
+            loop(1, 4, lambda k: third_copy(c, k, outer[c]).start())
+            core_copy(core, c, outer[c]).start()
+
+    def pass_on_third(sd):
+        if sd in (1, 2):
+            for k in (1, 3) if sd == 1 else (2,):
+                for c in range(2):
+                    owner = lax.rem(outer[c] + k, 4)
+                    third_copy(c, k, owner).wait_recv()
+                    core_copy(core, c, owner).start()
+
+    mixed = mixer(here, comp, sc["tokens"][...], cw, cb, ng, sc, pass_on_second, pass_on_third)
+    for c in range(2):
+        loop(0, 4, lambda q: core_copy(1 - core, c, q).wait_recv())
+    order = []
+    for s in range(32):
+        yy, zz, xx = s // 8, 4 * ((s // 4) % 2), s % 4
+        order += [(0, 4 * yy + xx, zz), (1, 4 * xx + yy, zz)]
     for low in range(4):
-        sides = [jnp.concatenate([wall[c, p, h + low] for p, h in order], axis=0) for c in range(2)]
+        sides = [jnp.concatenate([wall[k, c, p, zz + low] for c, p, zz in order], axis=0) for k in range(2)]
         out[:, 256 * low : 256 * low + 256] = dot(mixed, jnp.concatenate(sides, axis=1)).astype(BF16)
 
-    each(8, lambda k: z_copy(k, z, on_z(z_peer(k))).wait_send())
-    each(32, lambda k: token_copy(k, here, (batch, seq_peer(k))).wait_send())
-    each(16, lambda k: plane_copy(k, plane, on_plane(plane_peer(k))).wait_send())
-    lax.fori_loop(0, 16, lambda q, c: (core_copy(core, q).wait_send(), c)[1], 0)
+    for c in range(2):
+        loop(1, 8, lambda k: z_copy(c, k, z).wait_send())
+        loop(1, 4, lambda k: second_copy(c, k, inner[c]).wait_send())
+        loop(1, 4, lambda k: third_copy(c, k, outer[c]).wait_send())
+        loop(0, 4, lambda q: core_copy(core, c, q).wait_send())
+    loop(1, 32, lambda k: token_copy(k, here).wait_send())
 
 
 def on_device(tok, comp, emb, inw, stw, cw, cb, sb, dr, sg, ng, wout):
     params = [comp, emb, inw, stw.T, cw, cb, sb, dr, sg, ng]
     shapes = scratch(32)
     shapes["received"] = pltpu.VMEM((32, 1, BLOCK), jnp.int32)
-    shapes["wall"] = pltpu.VMEM((2, 16, 8, 32, 128), BF16)
-    shapes["own_sem"] = pltpu.SemaphoreType.DMA((2 + PARAMS,))
-    for name, count in (("token", 32), ("z", 8), ("plane", 16), ("core", 16)):
-        shapes[name + "_send"] = pltpu.SemaphoreType.DMA((count,))
-        shapes[name + "_recv"] = pltpu.SemaphoreType.DMA((count,))
+    shapes["wall"] = pltpu.VMEM((2, 2, 16, 8, 16, 128), BF16)
+    shapes["own_sem"] = pltpu.SemaphoreType.DMA((3 + PARAMS,))
+    for name, count in (("token", (32,)), ("z", (2, 8)), ("second", (2, 4)), ("third", (2, 4)), ("core", (2, 4))):
+        shapes[name + "_send"] = pltpu.SemaphoreType.DMA(count)
+        shapes[name + "_recv"] = pltpu.SemaphoreType.DMA(count)
     for i, value in enumerate(params):
         space = pltpu.SMEM if value.ndim == 1 else pltpu.VMEM
         shapes[f"held{i}"] = space(value.shape, value.dtype)

time: 38 us -> 35.5 us (0.934)
  Pallas kernels: 36 us -> 33.5 us
    pallas_call x1, Pallas kernels: 36 us -> 33.5 us  [on_device(): pl.pallas_call(partial(kernel, tuple(shapes)), out_shape=jax.ShapeDtypeSt...]
where the time goes in v3:
time: 35.5 us; the launch traced here: 35.4 us
  Pallas kernels  33.5 us (94%)
  local copies, waits for them, and re-layouts  1.87 us (5%)
    pallas_call x1, Pallas kernels, on_device(): pl.pallas_call(partial(kernel, tuple(shapes)), out_shape=jax.ShapeDtypeSt...  33.5 us
    unnamed x1, local copies, waits for them, and re-layouts  1.87 us

profile of v3, /device:TPU:1, one launch (start us, length us, event | category | flops | bytes accessed | tf_op | source)
XLA Modules:
  0.0 35.4 jit_solution(16975829607576623979)
XLA Ops:
  0.0 33.5 %shard_map.118 = bf16[256,1024]{1,0:T(8,128)(2,1)} custom-call(s32[4]{0:T(128)} %refs_0_.1, bf16[4,1024]{1,0:T(4,128)(2,1)} %refs_1_.1, bf16[1024,2176]{1,0:T(8,128)(2,1)} %refs_2_.1, bf16[16,1024]{1,0:T(8,128)(2,1)} %bitcast.3, f32[2,4,1152]{2,1,0:T(4,128)} %refs_4_.1, f32[2,1152]{1,0:T(2,128)} %refs_5_.1, f32[2,16]{1,0:T(2,128)} %refs_6_.1, ...), custom_call_target="tpu_custom_call" | custom-call | tf_op jit(solution)/shard_map/pallas_call | solution.py:540
  33.5 1.9 %copy.14 = bf16[1,256,1024]{2,1,0:T(8,128)(2,1)} copy(bf16[1,256,1024]{2,1,0:T(8,128)(2,1)} %bitcast.2) | data formatting | bytes 1048576

commit v4 on v3

--- a/solution.py
+++ b/solution.py
@@ -135,16 +135,56 @@
             size = size + coef[part, 8 + v : 9 + v] * hot[v : v + 1]
         sc["run"][part, :] = power
         sc["from"][part, :] = power - size
-        for v in range(8):
-            at = v if v < 4 else v + 4
-            sc["spread"][side, v] = jnp.broadcast_to(coef[part, at : at + 1], (32, 128))
+        k = iota((32, 48), 1)
+        factor = jnp.zeros((32, 48), F32)
+        for v in range(4):
+            decay, size = coef[part, v : v + 1], coef[part, 8 + v : 9 + v]
+            value = jnp.where(k < 16, 64.0 * decay, jnp.where(k < 32, decay, size))
+            factor = jnp.where(k % 4 == v, value, factor)
+        pieces = []
+        for _ in range(3):
+            pieces.append(factor.astype(BF16).astype(F32))
+            factor = factor - pieces[-1]
+        pieces = jnp.concatenate(pieces, axis=0)
+        block = (iota((96, 48), 1) // 4) % 4
+        for at in range(4):
+            sc["factor"][side, at] = jnp.where(block == at, pieces, 0.0).astype(BF16)
     sc["run_t"][...] = sc["run"][...].T
     letter = jnp.broadcast_to(mine.astype(F32), (128, BLOCK)).T.astype(jnp.int32)[:, 0:32]
     for strand in range(2):
         hit = jnp.where(iota((BLOCK, 32), 1) % 16 == letter + 8 * strand, 1.0, 0.0).astype(BF16)
         sc["gate"][strand] = dot(hit, sc["gate_parts"][...])
+    eye = iota((128, 128), 0) == iota((128, 128), 1)
     for d in range(2):
+        for h in range(H):
+            gain = sc["skip_rows"][4 + d : 5 + d, 64 * h : 64 * h + 1]
+            sc["skip_eye"][16 * d + h] = jnp.where(eye, gain, 0.0).astype(BF16)
         sc["b_columns"][d, :, 0:GRAMS] = sc["table"][d, 0:GRAMS, E:CH].astype(F32).T.astype(BF16)
+
+
+def local_conv(mine, comp, sc):
+    others = jnp.zeros_like(mine)
+    for v in range(4):
+        others = jnp.where(mine == v, comp[v], others)
+    lane = iota(mine.shape, 1)
+    words = []
+    for sd in range(4):
+        letters = others if STRAND[sd] else mine
+        word = letters
+        for k in (1, 2, 3):
+            word = word + 4**k * pltpu.roll(letters, k if RISING[sd] else BLOCK - k, axis=1)
+        inside = lane >= 3 if RISING[sd] else lane < BLOCK - 3
+        words.append(jnp.where(inside, word, -1).astype(F32))
+    words = jnp.concatenate(words + [jnp.zeros((124, BLOCK), F32)], axis=0).T.astype(jnp.int32)
+    for sd in range(4):
+        hit = jnp.where(iota((BLOCK, GRAMS), 1) == words[:, sd : sd + 1], 1.0, 0.0).astype(BF16)
+        sc["conved"][sd] = dot(hit, sc["table"][SET[sd], 0:GRAMS]).astype(BF16)
+    other_word = jnp.zeros((1, GRAMS), jnp.int32)
+    for place in (64, 16, 4, 1):
+        digit = (iota((1, GRAMS), 1) // place) % 4
+        for v in range(4):
+            other_word = other_word + jnp.where(digit == v, comp[v] * place, 0)
+    sc["swap"][...] = jnp.where(iota((GRAMS, GRAMS), 0) == other_word, 1.0, 0.0).astype(BF16)
 
 
 def local_decays(sd, sc):
@@ -173,7 +213,7 @@
         sc["grow"][sd, :, 128 * pair : 128 * pair + 128] = jnp.exp2(jnp.where(left, reached[0], reached[1]))
 
 
-def mixer(here, comp, tokens, cw_ref, cb_ref, ng_ref, sc, after_history, between_scans):
+def mixer(here, comp, tokens, cw_ref, cb_ref, ng_ref, sc, between_scans):
     blocks = tokens.shape[0]
     others = jnp.zeros_like(tokens)
     for v in range(4):
@@ -211,32 +251,27 @@
         edge_letters.append(columns)
     edge_tables(edge_letters, sc["conv_in"], cw_ref, cb_ref, sc["table"])
 
-    for v in range(4):
-        sc["one_hot"][v * blocks : (v + 1) * blocks, :] = jnp.where(tokens == v, 1.0, 0.0)
-    one_hot = sc["one_hot"][...]
+    rows = 4 * blocks
+    one_hot = jnp.where(sc["fourfold"][...] == iota((rows, BLOCK), 0) % 4, 1.0, 0.0)
     upper = jnp.where(iota((BLOCK, BLOCK), 0) <= iota((BLOCK, BLOCK), 1), 1.0, 0.0)
     inside = dot(one_hot.astype(BF16), upper.astype(BF16))
-    sc["inside"][...] = inside
     total = inside[:, BLOCK - 1 : BLOCK]
-    rows = 4 * blocks
     a, b = iota((rows, rows), 0), iota((rows, rows), 1)
-    aj, bj = a % blocks, b % blocks
-    between = (a // blocks == b // blocks) & (((aj < bj) & (bj < here)) | ((here < bj) & (bj < aj)))
+    aj, bj = a // 4, b // 4
+    between = (a % 4 == b % 4) & (((aj < bj) & (bj < here)) | ((here < bj) & (bj < aj)))
     passed = dot(jnp.where(between, 1.0, 0.0).astype(BF16), jnp.broadcast_to(total, inside.shape).astype(BF16))
-    before = iota((rows, 1), 0) % blocks < here
-    sc["away"][...] = passed + jnp.where(before, total - inside, inside - one_hot)
-
-    def entry_weights(j, side):
-        counts = [sc["away"][pl.ds(v * blocks + j, 1), :] for v in range(4)]
-        letter = [sc["one_hot"][pl.ds(v * blocks + j, 1), :] for v in range(4)]
-        halves = []
-        for lanes in (slice(0, 128), slice(128, 256)):
-            power = jnp.zeros((32, 128), F32)
-            for v in range(4):
-                power = power + sc["spread"][side, v] * counts[v][:, lanes]
-                power = power + sc["spread"][side, 4 + v] * letter[v][:, lanes]
-            halves.append(jnp.exp2(power))
-        return jnp.concatenate(halves, axis=1)
+    before = iota((rows, 1), 0) // 4 < here
+    away = passed + jnp.where(before, total - inside, inside - one_hot)
+    high = jnp.floor(away * (1.0 / 64.0))
+    sc["counts"][0] = high.astype(BF16)
+    sc["counts"][1] = (away - 64.0 * high).astype(BF16)
+    sc["counts"][2] = one_hot.astype(BF16)
+
+    def entry_weights(four, at, side):
+        start = 16 * four if isinstance(four, int) else pl.multiple_of(16 * four, 16)
+        counts = jnp.concatenate([sc["counts"][i, pl.ds(start, 16), :] for i in range(3)], axis=0)
+        power = dot(sc["factor"][side, at], counts)
+        return jnp.exp2(power[0:32] + power[32:64] + power[64:96])
 
     word_of_row = iota((GRAMS, BLOCK), 0).astype(F32).astype(BF16)
     group = 8
@@ -248,25 +283,19 @@
             side = jnp.where(j < here, 0, 1)
             words = sc["words"][2 * side, pl.ds(j, 1), :].astype(F32).astype(BF16)
             hits.append(jnp.where(word_of_row == words, jnp.ones((), BF16), jnp.zeros((), BF16)))
-            power = entry_weights(j, side)
+            power = entry_weights(step * (group // 4) + i // 4, i % 4, side)
             both = [jnp.where(j < here, power, 0.0), jnp.where(j > here, power, 0.0)]
             powers.append(jnp.concatenate(both, axis=0).astype(BF16))
         return acc + dot_t(jnp.concatenate(hits, axis=1), jnp.concatenate(powers, axis=1))
 
-    other_word = jnp.zeros((1, GRAMS), jnp.int32)
-    for place in (64, 16, 4, 1):
-        digit = (iota((1, GRAMS), 1) // place) % 4
-        for v in range(4):
-            other_word = other_word + jnp.where(digit == v, comp[v] * place, 0)
-    swap = jnp.where(iota((GRAMS, GRAMS), 0) == other_word, 1.0, 0.0).astype(BF16)
     acc = lax.fori_loop(0, blocks // group, entering, jnp.zeros((GRAMS, 64), F32)).astype(BF16)
-    swapped = dot(swap, acc)
+    swapped = dot(sc["swap"][...], acc)
     lane64 = iota((GRAMS, 64), 1)
     sc["weigh"][0:GRAMS, :] = jnp.where(lane64 % 32 < 16, acc.astype(F32), swapped).astype(BF16)
     edges = []
     for side in (0, 1):
         present = here > 0 if side == 0 else here < blocks - 1
-        edge = entry_weights(0 if side == 0 else blocks - 1, side)
+        edge = entry_weights(0, 0, 0) if side == 0 else entry_weights(blocks // 4 - 1, 3, 1)
         edges.append(jnp.where(present, edge, 0.0).astype(BF16))
     own = (iota((16, 32), 0) < 4) == (iota((16, 32), 1) < 16)
     for side in (0, 1):
@@ -286,52 +315,70 @@
         tail = jnp.concatenate([tail, jnp.zeros((112, CH - E), F32)], axis=0).T
         sc["b_columns"][d, :, GRAMS:ROWS] = tail[:, 0 : ROWS - GRAMS].astype(BF16)
 
-    after_history()
-    left = iota((BLOCK, 128), 1) < 64
-    half = BLOCK // 2
+    for d in range(2):
+        scans = [sd for sd in range(4) if SET[sd] == d]
+        hits = []
+        for sd in scans:
+            part = slice(0, 16) if RISING[sd] else slice(BLOCK - 16, BLOCK)
+            hits.append(jnp.where(iota((16, ROWS), 1) == local[part, sd : sd + 1], 1.0, 0.0))
+        rows = dot(jnp.concatenate(hits, axis=0).astype(BF16), sc["table"][d]).astype(BF16)
+        for i, sd in enumerate(scans):
+            part = slice(0, 16) if RISING[sd] else slice(BLOCK - 16, BLOCK)
+            sc["conved"][sd, part, :] = rows[16 * i : 16 * i + 16]
+
     for sd in range(4):
-        d, rising = SET[sd], RISING[sd]
-        hit = jnp.where(iota((BLOCK, ROWS), 1) == local[:, sd : sd + 1], 1.0, 0.0).astype(BF16)
-        conved = dot(hit, sc["table"][d])
-        sc["conved"][...] = conved.astype(BF16)
-        tail = conved[:, E:]
-        b_rows = tail[:, :64].astype(BF16)
-        c_rows = pltpu.roll(tail, 64, axis=1)[:, :64].astype(BF16)
-        sc["scores"][...] = dot_t(c_rows, b_rows).astype(BF16)
-
+        d = SET[sd]
+        tail = sc["conved"][sd, :, E:CH]
+        b_rows = tail[:, :64]
+        c_rows = pltpu.roll(tail.astype(F32), 64, axis=1)[:, :64].astype(BF16)
+        sc["scores"][sd] = dot_t(c_rows, b_rows).astype(BF16)
         place = jnp.where(iota((64, E), 0) == 16 * sd + iota((64, E), 1) // 64, 1.0, 0.0).astype(BF16)
         weights = dot(sc["weigh"][...], place)
         weighted = weights.astype(BF16) * sc["table"][d, :, 0:E]
         state = dot(sc["b_columns"][d, 0:64, :], weighted).astype(BF16)
-        sc["carried"][...] = dot(c_rows, state)
-
+        sc["carried"][sd] = dot(c_rows, state)
+
+    left = iota((BLOCK, 128), 1) < 64
+    half = BLOCK // 2
+    scales = []
+    for sd in range(4):
+        d, rising = SET[sd], RISING[sd]
         square = jnp.zeros((BLOCK, 128), F32)
         for pair in range(8):
             cols = slice(128 * pair, 128 * pair + 128)
-            values = sc["conved"][:, cols]
+            values = sc["conved"][sd, :, cols]
             parts = []
             for sub in range(2):
                 h = 16 * sd + 2 * pair + sub
+                skip = sc["skip_eye"][16 * d + 2 * pair + sub]
                 rows_of = []
                 for top in (True, False):
                     ts = slice(0, half) if top else slice(half, BLOCK)
-                    ss = slice(0, BLOCK) if top != rising else ts
-                    rows_of.append(dot(sc["decay"][h, ts, ss] * sc["scores"][ts, ss], values[ss]))
+                    mixing = sc["decay"][h, ts, ts] * sc["scores"][sd, ts, ts] + skip
+                    if top == rising:
+                        rows_of.append(dot(mixing, values[ts]))
+                    else:
+                        ss = slice(half, BLOCK) if top else slice(0, half)
+                        far = sc["decay"][h, ts, ss] * sc["scores"][sd, ts, ss]
+                        whole = [mixing, far] if top else [far, mixing]
+                        rows_of.append(dot(jnp.concatenate(whole, axis=1), values))
                 parts.append(jnp.concatenate(rows_of, axis=0))
-            both = jnp.where(left, parts[0], parts[1])
-            both = both + sc["carried"][:, cols] * sc["grow"][sd, :, cols]
-            both = both + sc["skip_rows"][4 + d : 5 + d, cols] * values.astype(F32)
+            both = jnp.where(left, parts[0], parts[1]) + sc["carried"][sd, :, cols] * sc["grow"][sd, :, cols]
             gated = both * sc["gate"][STRAND[sd], :, cols]
             square = square + gated * gated
-            sc["gated"][:, cols] = gated
+            sc["gated"][sd, :, cols] = gated
         mean = jnp.sum(square, axis=1, keepdims=True) * (1.0 / E)
-        normed = sc["gated"][...] * lax.rsqrt(mean + EPS) * ng_ref[d : d + 1, :]
-        if sd == 0:
-            sc["mixed"][...] = normed
-        else:
-            sc["mixed"][...] += normed
+        scales.append(lax.rsqrt(mean + EPS))
         between_scans(sd)
-    return sc["mixed"][...].astype(BF16)
+    for pair in range(8):
+        cols = slice(128 * pair, 128 * pair + 128)
+        ones, twos = [sc["gated"][0, :, cols] * scales[0], sc["gated"][3, :, cols] * scales[3]], [
+            sc["gated"][1, :, cols] * scales[1],
+            sc["gated"][2, :, cols] * scales[2],
+        ]
+        mixed = (ones[0] + ones[1]) * ng_ref[0:1, cols] + (twos[0] + twos[1]) * ng_ref[1:2, cols]
+        sc["mixed"][:, cols] = mixed.astype(BF16)
+    return sc["mixed"][...]
 
 
 def scratch(blocks):
@@ -344,26 +391,27 @@
         "s01": pltpu.VMEM((16, CH), F32),
         "s23": pltpu.VMEM((16, CH), F32),
         "table": pltpu.VMEM((2, ROWS, CH), BF16),
-        "one_hot": pltpu.VMEM((4 * blocks, BLOCK), F32),
-        "inside": pltpu.VMEM((4 * blocks, BLOCK), F32),
-        "away": pltpu.VMEM((4 * blocks, BLOCK), F32),
         "weigh": pltpu.VMEM((ROWS, 64), BF16),
         "edge": pltpu.VMEM((16, 64), F32),
-        "spread": pltpu.VMEM((2, 8, 32, 128), F32),
         "tokens": pltpu.VMEM((blocks, BLOCK), jnp.int32),
         "run": pltpu.VMEM((128, BLOCK), F32),
         "from": pltpu.VMEM((64, BLOCK), F32),
         "local": pltpu.VMEM((128, BLOCK), F32),
         "gate": pltpu.VMEM((2, BLOCK, E), F32),
-        "conved": pltpu.VMEM((BLOCK, CH), BF16),
-        "scores": pltpu.VMEM((BLOCK, BLOCK), BF16),
+        "conved": pltpu.VMEM((4, BLOCK, CH), BF16),
+        "scores": pltpu.VMEM((4, BLOCK, BLOCK), BF16),
+        "swap": pltpu.VMEM((GRAMS, GRAMS), BF16),
+        "skip_eye": pltpu.VMEM((32, 128, 128), BF16),
+        "factor": pltpu.VMEM((2, 4, 96, 48), BF16),
+        "counts": pltpu.VMEM((3, 4 * blocks, BLOCK), BF16),
+        "fourfold": pltpu.VMEM((4 * blocks, BLOCK), jnp.int32),
         "run_t": pltpu.VMEM((BLOCK, 128), F32),
         "b_columns": pltpu.VMEM((2, 128, ROWS), BF16),
         "decay": pltpu.VMEM((64, BLOCK, BLOCK), BF16),
         "grow": pltpu.VMEM((4, BLOCK, E), F32),
-        "carried": pltpu.VMEM((BLOCK, E), F32),
-        "gated": pltpu.VMEM((BLOCK, E), F32),
-        "mixed": pltpu.VMEM((BLOCK, E), F32),
+        "carried": pltpu.VMEM((4, BLOCK, E), F32),
+        "gated": pltpu.VMEM((4, BLOCK, E), F32),
+        "mixed": pltpu.VMEM((BLOCK, E), BF16),
     }
 
 
@@ -396,22 +444,24 @@
 
         lax.fori_loop(first, last, go, 0)
 
-    def greet_z(k):
-        greet((lax.rem(z_low + k, 4) * 2 + core, y * 8 + x))
-        greet((lax.rem(z_low + k, 4) * 2 + core, y * 8 + 4 + x))
-
-    loop(1, 32, lambda k: greet((batch, lax.rem(here + k, 32))))
-    loop(1, 4, greet_z)
+    loop(1, 8, lambda k: greet(at(x, y, lax.rem(z + k, 8))))
+    loop(1, 16, lambda k: greet((batch, lax.div(lax.rem(4 * y + x + k, 16), 4) * 8 + 4 * z_high + lax.rem(x + k, 4))))
     greet(partner)
 
     def copy_of(piece, send, recv, device):
         return pltpu.make_async_remote_copy(piece, piece, send, recv, device, MESH)
 
-    def seq_peer(k):
-        return lax.rem(here + k, 32)
-
-    def token_copy(k, owner):
-        return copy_of(received.at[owner], sc["token_send"].at[k], sc["token_recv"].at[owner], (batch, seq_peer(k)))
+    def token_z(owner):
+        piece = received.at[y, x, owner]
+        return copy_of(piece, sc["token_send"].at[0], sc["token_recv"].at[16], at(x, y, lax.rem(z + 4, 8)))
+
+    def plane_peer(k):
+        return lax.rem(4 * y + x + k, 16)
+
+    def token_plane(k, owner):
+        device = at(lax.rem(plane_peer(k), 4), lax.div(plane_peer(k), 4), z)
+        piece = received.at[lax.div(owner, 4), lax.rem(owner, 4)]
+        return copy_of(piece, sc["token_send"].at[k], sc["token_recv"].at[owner], device)
 
     mine, inner, outer = [y * 4 + x, x * 4 + y], [x, y], [y, x]
 
@@ -435,7 +485,7 @@
         piece = wall.at[side, c, pl.ds(4 * owner, 4)]
         return copy_of(piece, sc["core_send"].at[c, owner], sc["core_recv"].at[c, owner], partner)
 
-    first = [pltpu.make_async_copy(tok, received.at[here], sc["own_sem"].at[0])]
+    first = [pltpu.make_async_copy(tok, received.at[y, x, z_high], sc["own_sem"].at[0])]
     for c in range(2):
         half = shard.at[16 * c : 16 * c + 16]
         first.append(pltpu.make_async_copy(half, wall.at[core, c, mine[c], z], sc["own_sem"].at[1 + c]))
@@ -449,19 +499,11 @@
         copy.wait()
 
     def send():
-        pl.semaphore_wait(barrier, 38)
+        pl.semaphore_wait(barrier, 23)
+        token_z(z_high).start()
         for c in range(2):
             loop(1, 8, lambda k: z_copy(c, k, z).start())
-        loop(1, 32, lambda k: token_copy(k, here).start())
-
-    def pass_on_z():
-        for c in range(2):
-            loop(1, 8, lambda k: z_copy(c, k, lax.rem(z + k, 8)).wait_recv())
-            loop(1, 4, lambda k: second_copy(c, k, inner[c]).start())
-
-    distance = z + lax.min(y, 4 - y) + lax.min(x, 4 - x)
-    soon = (z_high == 0) & (distance < 4)
-    later = (z_high == 0) & (distance >= 4)
+
     last = z_high == 1
 
     pl.when(last)(send)
@@ -473,39 +515,36 @@
         comp, emb, inw, stw, (sb, dr, sg), sc["gate_parts"], sc["conv_in"], sc["coef"], sc["skip_rows"]
     )
     gram_tables(sc["conv_in"], cw, cb, sc["s01"], sc["s23"], sc["table"])
-    pl.when(later)(send)
-    local_counts(received[here], sc)
-    pl.when(last)(pass_on_z)
-    local_decays(0, sc)
-    local_decays(1, sc)
-    pl.when(later)(pass_on_z)
-    local_decays(2, sc)
-    local_decays(3, sc)
-
-    @pl.when(soon)
-    def _():
-        send()
-        pass_on_z()
-
-    loop(1, 32, lambda k: token_copy(k, seq_peer(k)).wait_recv())
+    pl.when(z_high == 0)(send)
+    local_counts(received[y, x, z_high], sc)
+    local_conv(received[y, x, z_high], comp, sc)
+    for sd in range(4):
+        local_decays(sd, sc)
+
+    token_z(1 - z_high).wait_recv()
+    loop(1, 16, lambda k: token_plane(k, 4 * y + x).start())
+    for c in range(2):
+        loop(1, 8, lambda k: z_copy(c, k, lax.rem(z + k, 8)).wait_recv())
+        loop(1, 4, lambda k: second_copy(c, k, inner[c]).start())
+    for c in range(2):
+        loop(1, 4, lambda k: second_copy(c, k, lax.rem(inner[c] + k, 4)).wait_recv())
+        loop(1, 4, lambda k: third_copy(c, k, outer[c]).start())
+        core_copy(core, c, outer[c]).start()
+    loop(1, 16, lambda k: token_plane(k, plane_peer(k)).wait_recv())
     for j in range(32):
-        sc["tokens"][j : j + 1, :] = received[j]
-
-    def pass_on_second():
-        for c in range(2):
-            loop(1, 4, lambda k: second_copy(c, k, lax.rem(inner[c] + k, 4)).wait_recv())
-            loop(1, 4, lambda k: third_copy(c, k, outer[c]).start())
-            core_copy(core, c, outer[c]).start()
+        line = received[j // 8, j % 4, (j // 4) % 2]
+        sc["tokens"][j : j + 1, :] = line
+        sc["fourfold"][4 * j : 4 * j + 4, :] = jnp.broadcast_to(line, (4, BLOCK))
 
     def pass_on_third(sd):
-        if sd in (1, 2):
-            for k in (1, 3) if sd == 1 else (2,):
+        if sd < 2:
+            for k in (1, 3) if sd == 0 else (2,):
                 for c in range(2):
                     owner = lax.rem(outer[c] + k, 4)
                     third_copy(c, k, owner).wait_recv()
                     core_copy(core, c, owner).start()
 
-    mixed = mixer(here, comp, sc["tokens"][...], cw, cb, ng, sc, pass_on_second, pass_on_third)
+    mixed = mixer(here, comp, sc["tokens"][...], cw, cb, ng, sc, pass_on_third)
     for c in range(2):
         loop(0, 4, lambda q: core_copy(1 - core, c, q).wait_recv())
     order = []
@@ -521,16 +560,17 @@
         loop(1, 4, lambda k: second_copy(c, k, inner[c]).wait_send())
         loop(1, 4, lambda k: third_copy(c, k, outer[c]).wait_send())
         loop(0, 4, lambda q: core_copy(core, c, q).wait_send())
-    loop(1, 32, lambda k: token_copy(k, here).wait_send())
+    token_z(z_high).wait_send()
+    loop(1, 16, lambda k: token_plane(k, 4 * y + x).wait_send())
 
 
 def on_device(tok, comp, emb, inw, stw, cw, cb, sb, dr, sg, ng, wout):
     params = [comp, emb, inw, stw.T, cw, cb, sb, dr, sg, ng]
     shapes = scratch(32)
-    shapes["received"] = pltpu.VMEM((32, 1, BLOCK), jnp.int32)
+    shapes["received"] = pltpu.VMEM((4, 4, 2, 1, BLOCK), jnp.int32)
     shapes["wall"] = pltpu.VMEM((2, 2, 16, 8, 16, 128), BF16)
     shapes["own_sem"] = pltpu.SemaphoreType.DMA((3 + PARAMS,))
-    for name, count in (("token", (32,)), ("z", (2, 8)), ("second", (2, 4)), ("third", (2, 4)), ("core", (2, 4))):
+    for name, count in (("token", (17,)), ("z", (2, 8)), ("second", (2, 4)), ("third", (2, 4)), ("core", (2, 4))):
         shapes[name + "_send"] = pltpu.SemaphoreType.DMA(count)
         shapes[name + "_recv"] = pltpu.SemaphoreType.DMA(count)
     for i, value in enumerate(params):

time: 35.5 us -> 33.4 us (0.941)
  Pallas kernels: 33.5 us -> 31.4 us
    pallas_call x1, Pallas kernels: 33.5 us -> 31.4 us  [on_device(): pl.pallas_call(partial(kernel, tuple(shapes)), out_shape=jax.ShapeDtypeSt...]
where the time goes in v4:
time: 33.4 us; the launch traced here: 33.3 us
  Pallas kernels  31.4 us (94%)
  local copies, waits for them, and re-layouts  1.87 us (6%)
    pallas_call x1, Pallas kernels, on_device(): pl.pallas_call(partial(kernel, tuple(shapes)), out_shape=jax.ShapeDtypeSt...  31.4 us
    unnamed x1, local copies, waits for them, and re-layouts  1.87 us

profile of v4, /device:TPU:1, one launch (start us, length us, event | category | flops | bytes accessed | tf_op | source)
XLA Modules:
  0.0 33.3 jit_solution(11738385092718716819)
XLA Ops:
  0.0 31.4 %shard_map.118 = bf16[256,1024]{1,0:T(8,128)(2,1)} custom-call(s32[4]{0:T(128)} %refs_0_.1, bf16[4,1024]{1,0:T(4,128)(2,1)} %refs_1_.1, bf16[1024,2176]{1,0:T(8,128)(2,1)} %refs_2_.1, bf16[16,1024]{1,0:T(8,128)(2,1)} %bitcast.3, f32[2,4,1152]{2,1,0:T(4,128)} %refs_4_.1, f32[2,1152]{1,0:T(2,128)} %refs_5_.1, f32[2,16]{1,0:T(2,128)} %refs_6_.1, ...), custom_call_target="tpu_custom_call" | custom-call | tf_op jit(solution)/shard_map/pallas_call | solution.py:580
  31.4 1.9 %copy.14 = bf16[1,256,1024]{2,1,0:T(8,128)(2,1)} copy(bf16[1,256,1024]{2,1,0:T(8,128)(2,1)} %bitcast.2) | data formatting | bytes 1048576

commit v5 on v4

--- a/solution.py
+++ b/solution.py
@@ -584,9 +584,9 @@
         out_specs=pl.BlockSpec(memory_space=pltpu.VMEM),
         scratch_shapes=list(shapes.values()),
         compiler_params=pltpu.CompilerParams(
-            collective_id=0, has_side_effects=True, vmem_limit_bytes=60 << 20
+            collective_id=0, has_side_effects=True, vmem_limit_bytes=44 << 20
         ),
-    )(*params, wout, tok)
+    )(*[pltpu.with_memory_space_constraint(v, pltpu.HBM) for v in (*params, wout, tok)])
     return out[None]
 
 

time: 33.4 us -> 31.5 us (0.943)
  local copies, waits for them, and re-layouts: 1.87 us -> 0.8 us
  Pallas kernels: 31.4 us -> 30.6 us
    unnamed x1, local copies, waits for them, and re-layouts: 1.87 us -> 0.8 us
    pallas_call x1, Pallas kernels: 31.4 us -> 30.6 us  [on_device(): pl.pallas_call(partial(kernel, tuple(shapes)), out_shape=jax.ShapeDtypeSt...]
where the time goes in v5:
time: 31.5 us; the launch traced here: 31.4 us
  Pallas kernels  30.6 us (97%)
  local copies, waits for them, and re-layouts  0.8 us (3%)
    pallas_call x1, Pallas kernels, on_device(): pl.pallas_call(partial(kernel, tuple(shapes)), out_shape=jax.ShapeDtypeSt...  30.6 us
    unnamed x1, local copies, waits for them, and re-layouts  0.8 us

profile of v5, /device:TPU:1, one launch (start us, length us, event | category | flops | bytes accessed | tf_op | source)
XLA Modules:
  0.0 31.4 jit_solution(5617069321321570074)
XLA Ops:
  0.0 30.6 %shard_map.118 = bf16[256,1024]{1,0:T(8,128)(2,1)S(1)} custom-call(s32[4]{0:T(128)} %refs_0_.1, bf16[4,1024]{1,0:T(4,128)(2,1)} %refs_1_.1, bf16[1024,2176]{1,0:T(8,128)(2,1)} %refs_2_.1, bf16[16,1024]{1,0:T(8,128)(2,1)} %bitcast.3, f32[2,4,1152]{2,1,0:T(4,128)} %refs_4_.1, f32[2,1152]{1,0:T(2,128)} %refs_5_.1, f32[2,16]{1,0:T(2,128)} %refs_6_.1, ...), custom_call_target="tpu_custom_call" | custom-call | tf_op jit(solution)/shard_map/pallas_call | solution.py:580
  30.6 0.8 %copy.14 = bf16[1,256,1024]{2,1,0:T(8,128)(2,1)} copy(bf16[1,256,1024]{2,1,0:T(8,128)(2,1)S(1)} %bitcast.2) | data formatting | bytes 1048576

commit v6 on v5

--- a/solution.py
+++ b/solution.py
@@ -274,7 +274,7 @@
         return jnp.exp2(power[0:32] + power[32:64] + power[64:96])
 
     word_of_row = iota((GRAMS, BLOCK), 0).astype(F32).astype(BF16)
-    group = 8
+    group = 16
 
     def entering(step, acc):
         hits, powers = [], []

time: 31.5 us -> 31.3 us (level)
  no operation moved by 1% of the time
where the time goes in v6:
time: 31.3 us; the launch traced here: 31.2 us
  Pallas kernels  30.4 us (97%)
  local copies, waits for them, and re-layouts  0.8 us (3%)
    pallas_call x1, Pallas kernels, on_device(): pl.pallas_call(partial(kernel, tuple(shapes)), out_shape=jax.ShapeDtypeSt...  30.4 us
    unnamed x1, local copies, waits for them, and re-layouts  0.8 us

profile of v6, /device:TPU:1, one launch (start us, length us, event | category | flops | bytes accessed | tf_op | source)
XLA Modules:
  0.0 31.2 jit_solution(8035937462098794135)
XLA Ops:
  0.0 30.4 %shard_map.118 = bf16[256,1024]{1,0:T(8,128)(2,1)S(1)} custom-call(s32[4]{0:T(128)} %refs_0_.1, bf16[4,1024]{1,0:T(4,128)(2,1)} %refs_1_.1, bf16[1024,2176]{1,0:T(8,128)(2,1)} %refs_2_.1, bf16[16,1024]{1,0:T(8,128)(2,1)} %bitcast.3, f32[2,4,1152]{2,1,0:T(4,128)} %refs_4_.1, f32[2,1152]{1,0:T(2,128)} %refs_5_.1, f32[2,16]{1,0:T(2,128)} %refs_6_.1, ...), custom_call_target="tpu_custom_call" | custom-call | tf_op jit(solution)/shard_map/pallas_call | solution.py:580
  30.4 0.8 %copy.14 = bf16[1,256,1024]{2,1,0:T(8,128)(2,1)} copy(bf16[1,256,1024]{2,1,0:T(8,128)(2,1)S(1)} %bitcast.2) | data formatting | bytes 1048576

commit v7 on v6

--- a/solution.py
+++ b/solution.py
@@ -213,7 +213,7 @@
         sc["grow"][sd, :, 128 * pair : 128 * pair + 128] = jnp.exp2(jnp.where(left, reached[0], reached[1]))
 
 
-def mixer(here, comp, tokens, cw_ref, cb_ref, ng_ref, sc, between_scans):
+def mixer(here, comp, tokens, cw_ref, cb_ref, ng_ref, sc, before_history, between_scans):
     blocks = tokens.shape[0]
     others = jnp.zeros_like(tokens)
     for v in range(4):
@@ -288,6 +288,7 @@
             powers.append(jnp.concatenate(both, axis=0).astype(BF16))
         return acc + dot_t(jnp.concatenate(hits, axis=1), jnp.concatenate(powers, axis=1))
 
+    before_history()
     acc = lax.fori_loop(0, blocks // group, entering, jnp.zeros((GRAMS, 64), F32)).astype(BF16)
     swapped = dot(sc["swap"][...], acc)
     lane64 = iota((GRAMS, 64), 1)
@@ -526,15 +527,17 @@
     for c in range(2):
         loop(1, 8, lambda k: z_copy(c, k, lax.rem(z + k, 8)).wait_recv())
         loop(1, 4, lambda k: second_copy(c, k, inner[c]).start())
-    for c in range(2):
-        loop(1, 4, lambda k: second_copy(c, k, lax.rem(inner[c] + k, 4)).wait_recv())
-        loop(1, 4, lambda k: third_copy(c, k, outer[c]).start())
-        core_copy(core, c, outer[c]).start()
     loop(1, 16, lambda k: token_plane(k, plane_peer(k)).wait_recv())
     for j in range(32):
         line = received[j // 8, j % 4, (j // 4) % 2]
         sc["tokens"][j : j + 1, :] = line
         sc["fourfold"][4 * j : 4 * j + 4, :] = jnp.broadcast_to(line, (4, BLOCK))
+
+    def pass_on_second():
+        for c in range(2):
+            loop(1, 4, lambda k: second_copy(c, k, lax.rem(inner[c] + k, 4)).wait_recv())
+            loop(1, 4, lambda k: third_copy(c, k, outer[c]).start())
+            core_copy(core, c, outer[c]).start()
 
     def pass_on_third(sd):
         if sd < 2:
@@ -544,7 +547,7 @@
                     third_copy(c, k, owner).wait_recv()
                     core_copy(core, c, owner).start()
 
-    mixed = mixer(here, comp, sc["tokens"][...], cw, cb, ng, sc, pass_on_third)
+    mixed = mixer(here, comp, sc["tokens"][...], cw, cb, ng, sc, pass_on_second, pass_on_third)
     for c in range(2):
         loop(0, 4, lambda q: core_copy(1 - core, c, q).wait_recv())
     order = []

time: 31.3 us -> 31 us (level)
  no operation moved by 1% of the time
where the time goes in v7:
time: 31 us; the launch traced here: 30.9 us
  Pallas kernels  30.1 us (97%)
  local copies, waits for them, and re-layouts  0.8 us (3%)
    pallas_call x1, Pallas kernels, on_device(): pl.pallas_call(partial(kernel, tuple(shapes)), out_shape=jax.ShapeDtypeSt...  30.1 us
    unnamed x1, local copies, waits for them, and re-layouts  0.8 us

profile of v7, /device:TPU:1, one launch (start us, length us, event | category | flops | bytes accessed | tf_op | source)
XLA Modules:
  0.0 30.9 jit_solution(15543503211146398902)
XLA Ops:
  0.0 30.1 %shard_map.118 = bf16[256,1024]{1,0:T(8,128)(2,1)S(1)} custom-call(s32[4]{0:T(128)} %refs_0_.1, bf16[4,1024]{1,0:T(4,128)(2,1)} %refs_1_.1, bf16[1024,2176]{1,0:T(8,128)(2,1)} %refs_2_.1, bf16[16,1024]{1,0:T(8,128)(2,1)} %bitcast.3, f32[2,4,1152]{2,1,0:T(4,128)} %refs_4_.1, f32[2,1152]{1,0:T(2,128)} %refs_5_.1, f32[2,16]{1,0:T(2,128)} %refs_6_.1, ...), custom_call_target="tpu_custom_call" | custom-call | tf_op jit(solution)/shard_map/pallas_call | solution.py:583
  30.1 0.8 %copy.14 = bf16[1,256,1024]{2,1,0:T(8,128)(2,1)} copy(bf16[1,256,1024]{2,1,0:T(8,128)(2,1)S(1)} %bitcast.2) | data formatting | bytes 1048576
